TPU v7x, 512 devices: a whole 4x8x8 slice. The times are simulated.
512 devices in a mesh: ax: 8 (over z_hi, x), az: 64 (over z_lo, y, core).
Axes of the slice: x: 4, y: 8, z: 8 (z_hi: 2, z_lo: 4; z = z_hi * 4 + z_lo), core: 2. Of those that a mesh axis runs over, the one named last changes fastest.
Arguments:
- state: float32 [4, 32, 512, 2048], P(None, 'ax', 'az'), may hold values from -6 to 6
- rotor_offset: int32 [1], replicated, may hold values from 136 to 375
- rotor_fraction: float32 [1], replicated, may hold values from 0 to 1
Outputs:
- new_state: float32 [4, 32, 512, 2048], P(None, 'ax', 'az')
All inputs are finite; a program needn't handle non-finite values.
Results may differ from a plain program's by a relative error of at most 0.00002.
Values sent between devices are 32-bit elements; how exact they have to be, the bound alone decides.
No kernel may reach another device: no remote copies, remote signals or barrier semaphores. Data moves between devices by JAX's collectives and lax.ppermute only.
A program may use at most 64 MiB of HBM per device.

v0:
```python
import jax
import jax.numpy as jnp
from jax import lax
from jax.sharding import PartitionSpec as P

step_size = 0.2
base_viscosity = 0.05
eddy_coeff = 0.05


def from_behind(block, axis, distance):
    devices = range(lax.axis_size(axis))
    route = [((i - distance) % len(devices), i) for i in devices]
    return lax.ppermute(block, axis, route)


def with_halo(cells, sides, width, closed):
    for axis, dim in sides:
        count = lax.axis_size(axis)
        ends = count if closed else count - 1
        head = lax.slice_in_dim(cells, 0, width, axis=dim)
        tail = lax.slice_in_dim(cells, cells.shape[dim] - width, cells.shape[dim], axis=dim)
        cells = jnp.concatenate(
            [
                lax.ppermute(tail, axis, [(i, (i + 1) % count) for i in range(ends)]),
                cells,
                lax.ppermute(head, axis, [((i + 1) % count, i) for i in range(ends)]),
            ],
            axis=dim,
        )
    return cells


def tendency(field, up_p, dn_p, up_t, dn_t, up_r, dn_r):
    grad_p = (up_p - dn_p) * 0.5
    grad_t = (up_t - dn_t) * 0.5
    grad_r = (up_r - dn_r) * 0.5
    second = up_p - 2.0 * field + dn_p + (up_t - 2.0 * field + dn_t) + (up_r - 2.0 * field + dn_r)
    strain = (
        jnp.sum(grad_p[:3] * grad_p[:3], axis=0)
        + jnp.sum(grad_t[:3] * grad_t[:3], axis=0)
        + jnp.sum(grad_r[:3] * grad_r[:3], axis=0)
    )
    viscous = base_viscosity + eddy_coeff * jnp.sqrt(strain)
    advect = field[0] * grad_p + field[1] * grad_t + field[2] * grad_r
    return viscous * second - advect


def radial_sides(field, ghost_rot, ghost_sta):
    inner = field.shape[3] // 2
    zero = jnp.zeros(field.shape[:3] + (1,), field.dtype)
    up_r = jnp.concatenate(
        [field[..., 1:inner], ghost_rot[..., None], field[..., inner + 1 :], zero], axis=3
    )
    dn_r = jnp.concatenate(
        [zero, field[..., : inner - 1], ghost_sta[..., None], field[..., inner:-1]], axis=3
    )
    return (up_r, dn_r)


def interface_ghosts(stator_layer, rotor_layer, offset, fraction):
    sector = stator_layer.shape[2]
    cycle_count = lax.axis_size("az")
    beside_all = sector * cycle_count
    moves = jnp.stack([offset % beside_all, (-offset - 1) % beside_all])
    whole_moves = moves // sector
    remains = moves % sector
    stacked = jnp.stack([stator_layer, rotor_layer])
    levels = (cycle_count - 1).bit_length()
    for level in range(levels):
        moved = from_behind(stacked, "az", cycle_count - (1 << level))
        taken = whole_moves // (1 << level) % 2 == 1
        stacked = jnp.where(taken[:, None, None, None], moved, stacked)
    following = from_behind(stacked, "az", cycle_count - 1)
    extended = jnp.concatenate([stacked, following], axis=3)
    window_rot = lax.dynamic_slice_in_dim(extended[0], remains[0], sector + 1, 2)
    window_sta = lax.dynamic_slice_in_dim(extended[1], remains[1], sector + 1, 2)
    ghost_rot = (1.0 - fraction) * window_rot[..., :sector] + fraction * window_rot[..., 1:]
    ghost_sta = fraction * window_sta[..., :sector] + (1.0 - fraction) * window_sta[..., 1:]
    return (ghost_rot, ghost_sta)


def evaluate(field, offset, fraction):
    inner = field.shape[3] // 2
    ghost_rot, ghost_sta = interface_ghosts(
        field[..., inner], field[..., inner - 1], offset, fraction
    )
    axial_ext = with_halo(field, (("ax", 1),), 1, False)
    sector_ext = with_halo(field, (("az", 2),), 1, True)
    up_p = axial_ext[:, 2:]
    dn_p = axial_ext[:, :-2]
    up_t = sector_ext[:, :, 2:]
    dn_t = sector_ext[:, :, :-2]
    up_r, dn_r = radial_sides(field, ghost_rot, ghost_sta)
    return tendency(field, up_p, dn_p, up_t, dn_t, up_r, dn_r)


def shards(state, rotor_offset, rotor_fraction):
    offset = rotor_offset[0]
    fraction = rotor_fraction[0]
    section = state + step_size * evaluate(state, offset, fraction)
    return 0.5 * (state + (section + step_size * evaluate(section, offset, fraction)))


def solution(mesh):
    return jax.shard_map(
        shards,
        mesh=mesh,
        in_specs=(P(None, "ax", "az", None), P(), P()),
        out_specs=P(None, "ax", "az", None),
        check_vma=False,
    )
```

profile of v0, /device:TPU:6, one launch (start us, length us, event | category | flops | bytes accessed | tf_op | source)
XLA Modules:
  0.0 180.9 jit_solution(294002045920872073)
XLA Ops:
  0.0 1.1 slice_reduce_fusion.3
  1.2 10.2 %collective-permute-start.4 = (f32[2,4,4,8]{3,2,1,0:T(4,128)S(1)}, f32[2,4,4,8]{3,2,1,0:T(4,128)S(1)}, u32[]{:S(2)}, u32[]{:S(2)}) collective-permute-start(f32[2,4,4,8]{3,2,1,0:T(4,128)S(1)} %pad_maximum_fusion.8), channel_id=1, source_target_pairs={{1,0},{2,1},{3,2},{4,3},{5,4},{6,5},{7,6},{8,7},{9,8},{10,9},{11,1... | collective-permute-start | bytes 3080 | tf_op jit(solution)/shard_map/ppermute | solution.py:14
  12.3 0.5 collective-permute-done.4
  12.9 3.2 %collective-permute-start.5 = (f32[2,4,4,8]{3,2,1,0:T(4,128)S(1)}, f32[2,4,4,8]{3,2,1,0:T(4,128)S(1)}, u32[]{:S(2)}, u32[]{:S(2)}) collective-permute-start(f32[2,4,4,8]{3,2,1,0:T(4,128)S(1)} %broadcast_select_fusion.1), channel_id=1, source_target_pairs={{2,0},{3,1},{4,2},{5,3},{6,4},{7,5},{8,6},{9,7},{10,8},{11,9},{12,... | collective-permute-start | bytes 3080 | tf_op jit(solution)/shard_map/ppermute | solution.py:14
  16.2 1.9 %fusion.47 = (f32[4,1,8,2048]{3,2,1,0:T(8,128)}, f32[4,1,8,2048]{3,2,1,0:T(8,128)}) fusion(f32[4,4,8,2048]{3,2,1,0:T(8,128)} %param.3), kind=kLoop, calls=%fused_computation.147 | loop fusion | bytes 1048576 | tf_op jit(solution)/shard_map/slice | solution.py:22
  18.0 2.7 %collective-permute-start = (f32[4,1,8,2048]{3,2,1,0:T(8,128)}, f32[4,1,8,2048]{3,2,1,0:T(8,128)}, u32[]{:S(2)}, u32[]{:S(2)}) collective-permute-start(f32[4,1,8,2048]{3,2,1,0:T(8,128)} %get-tuple-element.32), channel_id=1, source_target_pairs={{64,0},{128,64},{192,128},{256,192},{320,256},{384,320},{448,384},... | collective-permute-start | bytes 786440 | tf_op jit(solution)/shard_map/ppermute | solution.py:27
  20.8 9.1 %collective-permute-start.1 = (f32[4,1,8,2048]{3,2,1,0:T(8,128)}, f32[4,1,8,2048]{3,2,1,0:T(8,128)}, u32[]{:S(2)}, u32[]{:S(2)}) collective-permute-start(f32[4,1,8,2048]{3,2,1,0:T(8,128)} %get-tuple-element.31), channel_id=1, source_target_pairs={{0,64},{64,128},{128,192},{192,256},{256,320},{320,384},{384,448},... | collective-permute-start | bytes 786440 | tf_op jit(solution)/shard_map/ppermute | solution.py:25
  30.0 4.0 %collective-permute-start.6 = (f32[2,4,4,8]{3,2,1,0:T(4,128)S(1)}, f32[2,4,4,8]{3,2,1,0:T(4,128)S(1)}, u32[]{:S(2)}, u32[]{:S(2)}) collective-permute-start(f32[2,4,4,8]{3,2,1,0:T(4,128)S(1)} %broadcast_select_fusion.3), channel_id=1, source_target_pairs={{4,0},{5,1},{6,2},{7,3},{8,4},{9,5},{10,6},{11,7},{12,8},{13,9},{1... | collective-permute-start | bytes 3080 | tf_op jit(solution)/shard_map/ppermute | solution.py:14
  34.2 0.7 copy.49
  34.9 3.5 %collective-permute-start.2 = (f32[4,4,1,2048]{3,1,2,0:T(4,128)}, f32[4,4,1,2048]{3,1,2,0:T(4,128)}, u32[]{:S(2)}, u32[]{:S(2)}) collective-permute-start(f32[4,4,1,2048]{3,1,2,0:T(4,128)} %copy.49), channel_id=1, source_target_pairs={{1,0},{2,1},{3,2},{4,3},{5,4},{6,5},{7,6},{8,7},{9,8},{10,9},{11,1... | collective-permute-start | bytes 393224 | tf_op jit(solution)/shard_map/ppermute | solution.py:27
  38.4 0.7 copy.50
  39.1 2.0 %collective-permute-start.3 = (f32[4,4,1,2048]{3,1,2,0:T(4,128)}, f32[4,4,1,2048]{3,1,2,0:T(4,128)}, u32[]{:S(2)}, u32[]{:S(2)}) collective-permute-start(f32[4,4,1,2048]{3,1,2,0:T(4,128)} %copy.50), channel_id=1, source_target_pairs={{0,1},{1,2},{2,3},{3,4},{4,5},{5,6},{6,7},{7,8},{8,9},{9,10},{10,1... | collective-permute-start | bytes 393224 | tf_op jit(solution)/shard_map/ppermute | solution.py:25
  41.3 2.1 %collective-permute-start.7 = (f32[2,4,4,8]{3,2,1,0:T(4,128)S(1)}, f32[2,4,4,8]{3,2,1,0:T(4,128)S(1)}, u32[]{:S(2)}, u32[]{:S(2)}) collective-permute-start(f32[2,4,4,8]{3,2,1,0:T(4,128)S(1)} %broadcast_select_fusion.5), channel_id=1, source_target_pairs={{8,0},{9,1},{10,2},{11,3},{12,4},{13,5},{14,6},{15,7},{16,8},{17,9... | collective-permute-start | bytes 3080 | tf_op jit(solution)/shard_map/ppermute | solution.py:14
  43.4 0.9 multiply_bitcast_fusion.2
  44.3 6.5 %collective-permute-done.7 = f32[2,4,4,8]{3,2,1,0:T(4,128)S(1)} collective-permute-done((f32[2,4,4,8]{3,2,1,0:T(4,128)S(1)}, f32[2,4,4,8]{3,2,1,0:T(4,128)S(1)}, u32[]{:S(2)}, u32[]{:S(2)}) %collective-permute-start.7) | collective-permute-done | bytes 1056 | tf_op jit(solution)/shard_map/ppermute | solution.py:14
  50.9 1.9 %collective-permute-start.8 = (f32[2,4,4,8]{3,2,1,0:T(4,128)S(1)}, f32[2,4,4,8]{3,2,1,0:T(4,128)S(1)}, u32[]{:S(2)}, u32[]{:S(2)}) collective-permute-start(f32[2,4,4,8]{3,2,1,0:T(4,128)S(1)} %broadcast_select_fusion.7), channel_id=1, source_target_pairs={{16,0},{17,1},{18,2},{19,3},{20,4},{21,5},{22,6},{23,7},{24,8},{25... | collective-permute-start | bytes 3080 | tf_op jit(solution)/shard_map/ppermute | solution.py:14
  52.8 1.4 fusion.49
  54.1 2.5 %collective-permute-done.8 = f32[2,4,4,8]{3,2,1,0:T(4,128)S(1)} collective-permute-done((f32[2,4,4,8]{3,2,1,0:T(4,128)S(1)}, f32[2,4,4,8]{3,2,1,0:T(4,128)S(1)}, u32[]{:S(2)}, u32[]{:S(2)}) %collective-permute-start.8) | collective-permute-done | bytes 1056 | tf_op jit(solution)/shard_map/ppermute | solution.py:14
  56.7 1.9 %collective-permute-start.9 = (f32[2,4,4,8]{3,2,1,0:T(4,128)S(1)}, f32[2,4,4,8]{3,2,1,0:T(4,128)S(1)}, u32[]{:S(2)}, u32[]{:S(2)}) collective-permute-start(f32[2,4,4,8]{3,2,1,0:T(4,128)S(1)} %broadcast_select_fusion.9), channel_id=1, source_target_pairs={{32,0},{33,1},{34,2},{35,3},{36,4},{37,5},{38,6},{39,7},{40,8},{41... | collective-permute-start | bytes 3080 | tf_op jit(solution)/shard_map/ppermute | solution.py:14
  58.6 0.6 fusion.50
  63.7 9.5 %collective-permute-start.10 = (f32[2,4,4,8]{3,2,1,0:T(4,128)S(1)}, f32[2,4,4,8]{3,2,1,0:T(4,128)S(1)}, u32[]{:S(2)}, u32[]{:S(2)}) collective-permute-start(f32[2,4,4,8]{3,2,1,0:T(4,128)S(1)} %broadcast_select_fusion.11), channel_id=1, source_target_pairs={{1,0},{2,1},{3,2},{4,3},{5,4},{6,5},{7,6},{8,7},{9,8},{10,9},{11,1... | collective-permute-start | bytes 3080 | tf_op jit(solution)/shard_map/ppermute | solution.py:14
  73.2 1.4 collective-permute-done.10
  75.0 0.8 copy.42
  76.0 1.3 concatenate.110
  77.3 1.3 concatenate.109
  78.8 0.8 copy-done.1
  79.7 1.0 copy.38
  80.8 1.0 copy.40
  81.8 1.5 fusion.2
  83.6 1.0 copy-done.2
  84.8 2.1 %multiply_add_fusion = f32[4,4,8,2048]{3,2,1,0:T(8,128)S(1)} fusion(f32[4,4,8,2048]{3,2,1,0:T(8,128)S(1)} %copy-done, f32[4,4,8,2048]{3,2,1,0:T(8,128)S(1)} %sub.89, f32[4,4,8,2048]{3,2,1,0:T(8,128)S(1)} %concatenate.110, f32[4,4,8,2048]{3,2,1,0:T(8,128)S(1)} %copy-done.2, f32[4,4,1,2048]{3,2,1,0:T(1,128)S(1)} %copy.38, f32[4,4,1,2048]{3,2,1,0:T(1,128)S(1)} %copy.40, ...), kind=kLoop, calls=%fused_computation.11 | loop fusion | flops 6291456 | bytes 7077888 | tf_op jit(solution)/shard_map/add | solution.py:101
  86.8 0.2 slice_reduce_fusion.1
  87.0 7.5 %collective-permute-start.15 = (f32[2,4,4,8]{3,2,1,0:T(4,128)S(1)}, f32[2,4,4,8]{3,2,1,0:T(4,128)S(1)}, u32[]{:S(2)}, u32[]{:S(2)}) collective-permute-start(f32[2,4,4,8]{3,2,1,0:T(4,128)S(1)} %pad_maximum_fusion.9), channel_id=1, source_target_pairs={{1,0},{2,1},{3,2},{4,3},{5,4},{6,5},{7,6},{8,7},{9,8},{10,9},{11,1... | collective-permute-start | bytes 3080 | tf_op jit(solution)/shard_map/ppermute | solution.py:14
  94.6 1.4 collective-permute-done.15
  96.1 1.9 %collective-permute-start.16 = (f32[2,4,4,8]{3,2,1,0:T(4,128)S(1)}, f32[2,4,4,8]{3,2,1,0:T(4,128)S(1)}, u32[]{:S(2)}, u32[]{:S(2)}) collective-permute-start(f32[2,4,4,8]{3,2,1,0:T(4,128)S(1)} %broadcast_select_fusion), channel_id=1, source_target_pairs={{2,0},{3,1},{4,2},{5,3},{6,4},{7,5},{8,6},{9,7},{10,8},{11,9},{12,... | collective-permute-start | bytes 3080 | tf_op jit(solution)/shard_map/ppermute | solution.py:14
  98.0 3.7 %collective-permute-done.16 = f32[2,4,4,8]{3,2,1,0:T(4,128)S(1)} collective-permute-done((f32[2,4,4,8]{3,2,1,0:T(4,128)S(1)}, f32[2,4,4,8]{3,2,1,0:T(4,128)S(1)}, u32[]{:S(2)}, u32[]{:S(2)}) %collective-permute-start.16) | collective-permute-done | bytes 1056 | tf_op jit(solution)/shard_map/ppermute | solution.py:14
  101.8 2.0 %collective-permute-start.17 = (f32[2,4,4,8]{3,2,1,0:T(4,128)S(1)}, f32[2,4,4,8]{3,2,1,0:T(4,128)S(1)}, u32[]{:S(2)}, u32[]{:S(2)}) collective-permute-start(f32[2,4,4,8]{3,2,1,0:T(4,128)S(1)} %broadcast_select_fusion.2), channel_id=1, source_target_pairs={{4,0},{5,1},{6,2},{7,3},{8,4},{9,5},{10,6},{11,7},{12,8},{13,9},{1... | collective-permute-start | bytes 3080 | tf_op jit(solution)/shard_map/ppermute | solution.py:14
  104.0 4.4 %collective-permute-done.17 = f32[2,4,4,8]{3,2,1,0:T(4,128)S(1)} collective-permute-done((f32[2,4,4,8]{3,2,1,0:T(4,128)S(1)}, f32[2,4,4,8]{3,2,1,0:T(4,128)S(1)}, u32[]{:S(2)}, u32[]{:S(2)}) %collective-permute-start.17) | collective-permute-done | bytes 1056 | tf_op jit(solution)/shard_map/ppermute | solution.py:14
  108.5 1.9 %collective-permute-start.18 = (f32[2,4,4,8]{3,2,1,0:T(4,128)S(1)}, f32[2,4,4,8]{3,2,1,0:T(4,128)S(1)}, u32[]{:S(2)}, u32[]{:S(2)}) collective-permute-start(f32[2,4,4,8]{3,2,1,0:T(4,128)S(1)} %broadcast_select_fusion.4), channel_id=1, source_target_pairs={{8,0},{9,1},{10,2},{11,3},{12,4},{13,5},{14,6},{15,7},{16,8},{17,9... | collective-permute-start | bytes 3080 | tf_op jit(solution)/shard_map/ppermute | solution.py:14
  110.4 0.9 fusion.20
  111.3 6.7 %collective-permute-done.18 = f32[2,4,4,8]{3,2,1,0:T(4,128)S(1)} collective-permute-done((f32[2,4,4,8]{3,2,1,0:T(4,128)S(1)}, f32[2,4,4,8]{3,2,1,0:T(4,128)S(1)}, u32[]{:S(2)}, u32[]{:S(2)}) %collective-permute-start.18) | collective-permute-done | bytes 1056 | tf_op jit(solution)/shard_map/ppermute | solution.py:14
  118.1 1.9 %collective-permute-start.19 = (f32[2,4,4,8]{3,2,1,0:T(4,128)S(1)}, f32[2,4,4,8]{3,2,1,0:T(4,128)S(1)}, u32[]{:S(2)}, u32[]{:S(2)}) collective-permute-start(f32[2,4,4,8]{3,2,1,0:T(4,128)S(1)} %broadcast_select_fusion.6), channel_id=1, source_target_pairs={{16,0},{17,1},{18,2},{19,3},{20,4},{21,5},{22,6},{23,7},{24,8},{25... | collective-permute-start | bytes 3080 | tf_op jit(solution)/shard_map/ppermute | solution.py:14
  120.0 0.8 fusion.44
  120.9 2.9 %collective-permute-done.19 = f32[2,4,4,8]{3,2,1,0:T(4,128)S(1)} collective-permute-done((f32[2,4,4,8]{3,2,1,0:T(4,128)S(1)}, f32[2,4,4,8]{3,2,1,0:T(4,128)S(1)}, u32[]{:S(2)}, u32[]{:S(2)}) %collective-permute-start.19) | collective-permute-done | bytes 1056 | tf_op jit(solution)/shard_map/ppermute | solution.py:14
  123.8 1.9 %collective-permute-start.20 = (f32[2,4,4,8]{3,2,1,0:T(4,128)S(1)}, f32[2,4,4,8]{3,2,1,0:T(4,128)S(1)}, u32[]{:S(2)}, u32[]{:S(2)}) collective-permute-start(f32[2,4,4,8]{3,2,1,0:T(4,128)S(1)} %broadcast_select_fusion.8), channel_id=1, source_target_pairs={{32,0},{33,1},{34,2},{35,3},{36,4},{37,5},{38,6},{39,7},{40,8},{41... | collective-permute-start | bytes 3080 | tf_op jit(solution)/shard_map/ppermute | solution.py:14
  125.7 1.6 fusion.46
  127.3 1.9 %collective-permute-start.11 = (f32[4,1,8,2048]{3,2,1,0:T(8,128)}, f32[4,1,8,2048]{3,2,1,0:T(8,128)}, u32[]{:S(2)}, u32[]{:S(2)}) collective-permute-start(f32[4,1,8,2048]{3,2,1,0:T(8,128)} %get-tuple-element.19), channel_id=1, source_target_pairs={{64,0},{128,64},{192,128},{256,192},{320,256},{384,320},{448,384},... | collective-permute-start | bytes 786440 | tf_op jit(solution)/shard_map/ppermute | solution.py:27
  129.3 9.9 %collective-permute-start.12 = (f32[4,1,8,2048]{3,2,1,0:T(8,128)}, f32[4,1,8,2048]{3,2,1,0:T(8,128)}, u32[]{:S(2)}, u32[]{:S(2)}) collective-permute-start(f32[4,1,8,2048]{3,2,1,0:T(8,128)} %get-tuple-element.18), channel_id=1, source_target_pairs={{0,64},{64,128},{128,192},{192,256},{256,320},{320,384},{384,448},... | collective-permute-start | bytes 786440 | tf_op jit(solution)/shard_map/ppermute | solution.py:25
  139.2 0.7 copy.43
  139.9 14.7 %collective-permute-start.13 = (f32[4,4,1,2048]{3,1,2,0:T(4,128)}, f32[4,4,1,2048]{3,1,2,0:T(4,128)}, u32[]{:S(2)}, u32[]{:S(2)}) collective-permute-start(f32[4,4,1,2048]{3,1,2,0:T(4,128)} %copy.43), channel_id=1, source_target_pairs={{1,0},{2,1},{3,2},{4,3},{5,4},{6,5},{7,6},{8,7},{9,8},{10,9},{11,1... | collective-permute-start | bytes 393224 | tf_op jit(solution)/shard_map/ppermute | solution.py:27
  154.6 0.7 copy.45
  155.3 1.9 %collective-permute-start.14 = (f32[4,4,1,2048]{3,1,2,0:T(4,128)}, f32[4,4,1,2048]{3,1,2,0:T(4,128)}, u32[]{:S(2)}, u32[]{:S(2)}) collective-permute-start(f32[4,4,1,2048]{3,1,2,0:T(4,128)} %copy.45), channel_id=1, source_target_pairs={{0,1},{1,2},{2,3},{3,4},{4,5},{5,6},{6,7},{7,8},{8,9},{9,10},{10,1... | collective-permute-start | bytes 393224 | tf_op jit(solution)/shard_map/ppermute | solution.py:25
  157.3 7.5 %collective-permute-start.21 = (f32[2,4,4,8]{3,2,1,0:T(4,128)S(1)}, f32[2,4,4,8]{3,2,1,0:T(4,128)S(1)}, u32[]{:S(2)}, u32[]{:S(2)}) collective-permute-start(f32[2,4,4,8]{3,2,1,0:T(4,128)S(1)} %broadcast_select_fusion.10), channel_id=1, source_target_pairs={{1,0},{2,1},{3,2},{4,3},{5,4},{6,5},{7,6},{8,7},{9,8},{10,9},{11,1... | collective-permute-start | bytes 3080 | tf_op jit(solution)/shard_map/ppermute | solution.py:14
  164.9 1.4 collective-permute-done.21
  166.6 0.8 copy.48
  167.6 1.6 concatenate.117
  169.2 2.1 %concatenate.116 = f32[4,4,8,2048]{3,2,1,0:T(8,128)} concatenate(f32[4,4,8,1023]{3,2,1,0:T(8,128)} %get-tuple-element.25, f32[4,4,8,1]{3,2,1,0:T(8,128)S(1)} %copy.47, f32[4,4,8,1023]{3,2,1,0:T(8,128)} %get-tuple-element.24, f32[4,4,8,1]{3,2,1,0:T(8,128)S(1)} %broadcast.532), dimensions={3} | concatenate | bytes 2097152 | tf_op jit(solution)/shard_map/concatenate | solution.py:52
  171.3 1.3 sub.96
  172.7 1.0 copy.44
  173.8 1.0 copy.46
  174.8 1.5 fusion.3
  176.7 0.6 copy-done.6
  177.4 0.4 copy-done.3
  177.8 3.1 %add_multiply_fusion = f32[4,4,8,2048]{3,2,1,0:T(8,128)} fusion(f32[4,4,8,2048]{3,2,1,0:T(8,128)S(1)} %copy-done, f32[4,4,8,2048]{3,2,1,0:T(8,128)S(1)} %multiply_add_fusion, f32[4,4,8,2048]{3,2,1,0:T(8,128)S(1)} %sub.96, f32[4,4,8,2048]{3,2,1,0:T(8,128)S(1)} %concatenate.117, f32[4,4,8,2048]{3,2,1,0:T(8,128)S(1)} %copy-done.3, ...), kind=kLoop, calls=%fused_computation.8 | loop fusion | flops 6815744 | bytes 8126464 | tf_op jit(solution)/shard_map/mul | solution.py:102
  (73 shorter events, 3.6 us)
Async XLA Ops:
  0.0 34.0 %copy-start = (f32[4,4,8,2048]{3,2,1,0:T(8,128)S(1)}, f32[4,4,8,2048]{3,2,1,0:T(8,128)}, u32[]{:S(2)}) copy-start(f32[4,4,8,2048]{3,2,1,0:T(8,128)} %param.3) | copy-start | bytes 3145732
  1.2 11.7 %collective-permute-start.4 = (f32[2,4,4,8]{3,2,1,0:T(4,128)S(1)}, f32[2,4,4,8]{3,2,1,0:T(4,128)S(1)}, u32[]{:S(2)}, u32[]{:S(2)}) collective-permute-start(f32[2,4,4,8]{3,2,1,0:T(4,128)S(1)} %pad_maximum_fusion.8), channel_id=1, source_target_pairs={{1,0},{2,1},{3,2},{4,3},{5,4},{6,5},{7,6},{8,7},{9,8},{10,9},{11,1... | collective-permute-start | bytes 3080 | tf_op jit(solution)/shard_map/ppermute | solution.py:14
  12.3 17.6 %copy-start.10 = (pred[2]{0:T(512)(128)(4,1)}, pred[2]{0:T(512)(128)(4,1)S(1)}, u32[]{:S(2)}) copy-start(pred[2]{0:T(512)(128)(4,1)S(1)} %get-tuple-element.44) | copy-start | bytes 10
  12.3 28.9 %copy-start.8 = (pred[2]{0:T(512)(128)(4,1)}, pred[2]{0:T(512)(128)(4,1)S(1)}, u32[]{:S(2)}) copy-start(pred[2]{0:T(512)(128)(4,1)S(1)} %get-tuple-element.45) | copy-start | bytes 10
  12.9 17.0 %collective-permute-start.5 = (f32[2,4,4,8]{3,2,1,0:T(4,128)S(1)}, f32[2,4,4,8]{3,2,1,0:T(4,128)S(1)}, u32[]{:S(2)}, u32[]{:S(2)}) collective-permute-start(f32[2,4,4,8]{3,2,1,0:T(4,128)S(1)} %broadcast_select_fusion.1), channel_id=1, source_target_pairs={{2,0},{3,1},{4,2},{5,3},{6,4},{7,5},{8,6},{9,7},{10,8},{11,9},{12,... | collective-permute-start | bytes 3080 | tf_op jit(solution)/shard_map/ppermute | solution.py:14
  18.0 63.8 %collective-permute-start = (f32[4,1,8,2048]{3,2,1,0:T(8,128)}, f32[4,1,8,2048]{3,2,1,0:T(8,128)}, u32[]{:S(2)}, u32[]{:S(2)}) collective-permute-start(f32[4,1,8,2048]{3,2,1,0:T(8,128)} %get-tuple-element.32), channel_id=1, source_target_pairs={{64,0},{128,64},{192,128},{256,192},{320,256},{384,320},{448,384},... | collective-permute-start | bytes 786440 | tf_op jit(solution)/shard_map/ppermute | solution.py:27
  20.8 61.1 %collective-permute-start.1 = (f32[4,1,8,2048]{3,2,1,0:T(8,128)}, f32[4,1,8,2048]{3,2,1,0:T(8,128)}, u32[]{:S(2)}, u32[]{:S(2)}) collective-permute-start(f32[4,1,8,2048]{3,2,1,0:T(8,128)} %get-tuple-element.31), channel_id=1, source_target_pairs={{0,64},{64,128},{128,192},{192,256},{256,320},{320,384},{384,448},... | collective-permute-start | bytes 786440 | tf_op jit(solution)/shard_map/ppermute | solution.py:25
  30.0 11.2 %collective-permute-start.6 = (f32[2,4,4,8]{3,2,1,0:T(4,128)S(1)}, f32[2,4,4,8]{3,2,1,0:T(4,128)S(1)}, u32[]{:S(2)}, u32[]{:S(2)}) collective-permute-start(f32[2,4,4,8]{3,2,1,0:T(4,128)S(1)} %broadcast_select_fusion.3), channel_id=1, source_target_pairs={{4,0},{5,1},{6,2},{7,3},{8,4},{9,5},{10,6},{11,7},{12,8},{13,9},{1... | collective-permute-start | bytes 3080 | tf_op jit(solution)/shard_map/ppermute | solution.py:14
  34.9 44.8 %collective-permute-start.2 = (f32[4,4,1,2048]{3,1,2,0:T(4,128)}, f32[4,4,1,2048]{3,1,2,0:T(4,128)}, u32[]{:S(2)}, u32[]{:S(2)}) collective-permute-start(f32[4,4,1,2048]{3,1,2,0:T(4,128)} %copy.49), channel_id=1, source_target_pairs={{1,0},{2,1},{3,2},{4,3},{5,4},{6,5},{7,6},{8,7},{9,8},{10,9},{11,1... | collective-permute-start | bytes 393224 | tf_op jit(solution)/shard_map/ppermute | solution.py:27
  39.1 41.6 %collective-permute-start.3 = (f32[4,4,1,2048]{3,1,2,0:T(4,128)}, f32[4,4,1,2048]{3,1,2,0:T(4,128)}, u32[]{:S(2)}, u32[]{:S(2)}) collective-permute-start(f32[4,4,1,2048]{3,1,2,0:T(4,128)} %copy.50), channel_id=1, source_target_pairs={{0,1},{1,2},{2,3},{3,4},{4,5},{5,6},{6,7},{7,8},{8,9},{9,10},{10,1... | collective-permute-start | bytes 393224 | tf_op jit(solution)/shard_map/ppermute | solution.py:25
  41.3 9.5 %collective-permute-start.7 = (f32[2,4,4,8]{3,2,1,0:T(4,128)S(1)}, f32[2,4,4,8]{3,2,1,0:T(4,128)S(1)}, u32[]{:S(2)}, u32[]{:S(2)}) collective-permute-start(f32[2,4,4,8]{3,2,1,0:T(4,128)S(1)} %broadcast_select_fusion.5), channel_id=1, source_target_pairs={{8,0},{9,1},{10,2},{11,3},{12,4},{13,5},{14,6},{15,7},{16,8},{17,9... | collective-permute-start | bytes 3080 | tf_op jit(solution)/shard_map/ppermute | solution.py:14
  50.9 5.8 %collective-permute-start.8 = (f32[2,4,4,8]{3,2,1,0:T(4,128)S(1)}, f32[2,4,4,8]{3,2,1,0:T(4,128)S(1)}, u32[]{:S(2)}, u32[]{:S(2)}) collective-permute-start(f32[2,4,4,8]{3,2,1,0:T(4,128)S(1)} %broadcast_select_fusion.7), channel_id=1, source_target_pairs={{16,0},{17,1},{18,2},{19,3},{20,4},{21,5},{22,6},{23,7},{24,8},{25... | collective-permute-start | bytes 3080 | tf_op jit(solution)/shard_map/ppermute | solution.py:14
  56.7 6.9 %collective-permute-start.9 = (f32[2,4,4,8]{3,2,1,0:T(4,128)S(1)}, f32[2,4,4,8]{3,2,1,0:T(4,128)S(1)}, u32[]{:S(2)}, u32[]{:S(2)}) collective-permute-start(f32[2,4,4,8]{3,2,1,0:T(4,128)S(1)} %broadcast_select_fusion.9), channel_id=1, source_target_pairs={{32,0},{33,1},{34,2},{35,3},{36,4},{37,5},{38,6},{39,7},{40,8},{41... | collective-permute-start | bytes 3080 | tf_op jit(solution)/shard_map/ppermute | solution.py:14
  63.7 10.9 %collective-permute-start.10 = (f32[2,4,4,8]{3,2,1,0:T(4,128)S(1)}, f32[2,4,4,8]{3,2,1,0:T(4,128)S(1)}, u32[]{:S(2)}, u32[]{:S(2)}) collective-permute-start(f32[2,4,4,8]{3,2,1,0:T(4,128)S(1)} %broadcast_select_fusion.11), channel_id=1, source_target_pairs={{1,0},{2,1},{3,2},{4,3},{5,4},{6,5},{7,6},{8,7},{9,8},{10,9},{11,1... | collective-permute-start | bytes 3080 | tf_op jit(solution)/shard_map/ppermute | solution.py:14
  78.6 1.0 copy-start.1
  83.4 1.2 copy-start.2
  83.5 1.2 copy-start.4
  83.5 1.3 copy-start.5
  87.0 14.7 %copy-start.11 = (pred[2]{0:T(512)(128)(4,1)S(1)}, pred[2]{0:T(512)(128)(4,1)}, u32[]{:S(2)}) copy-start(pred[2]{0:T(512)(128)(4,1)} %copy-done.10) | copy-start | bytes 10
  87.0 9.0 %collective-permute-start.15 = (f32[2,4,4,8]{3,2,1,0:T(4,128)S(1)}, f32[2,4,4,8]{3,2,1,0:T(4,128)S(1)}, u32[]{:S(2)}, u32[]{:S(2)}) collective-permute-start(f32[2,4,4,8]{3,2,1,0:T(4,128)S(1)} %pad_maximum_fusion.9), channel_id=1, source_target_pairs={{1,0},{2,1},{3,2},{4,3},{5,4},{6,5},{7,6},{8,7},{9,8},{10,9},{11,1... | collective-permute-start | bytes 3080 | tf_op jit(solution)/shard_map/ppermute | solution.py:14
  96.1 5.6 %collective-permute-start.16 = (f32[2,4,4,8]{3,2,1,0:T(4,128)S(1)}, f32[2,4,4,8]{3,2,1,0:T(4,128)S(1)}, u32[]{:S(2)}, u32[]{:S(2)}) collective-permute-start(f32[2,4,4,8]{3,2,1,0:T(4,128)S(1)} %broadcast_select_fusion), channel_id=1, source_target_pairs={{2,0},{3,1},{4,2},{5,3},{6,4},{7,5},{8,6},{9,7},{10,8},{11,9},{12,... | collective-permute-start | bytes 3080 | tf_op jit(solution)/shard_map/ppermute | solution.py:14
  101.8 6.7 %copy-start.9 = (pred[2]{0:T(512)(128)(4,1)S(1)}, pred[2]{0:T(512)(128)(4,1)}, u32[]{:S(2)}) copy-start(pred[2]{0:T(512)(128)(4,1)} %copy-done.8) | copy-start | bytes 10
  101.8 6.7 %collective-permute-start.17 = (f32[2,4,4,8]{3,2,1,0:T(4,128)S(1)}, f32[2,4,4,8]{3,2,1,0:T(4,128)S(1)}, u32[]{:S(2)}, u32[]{:S(2)}) collective-permute-start(f32[2,4,4,8]{3,2,1,0:T(4,128)S(1)} %broadcast_select_fusion.2), channel_id=1, source_target_pairs={{4,0},{5,1},{6,2},{7,3},{8,4},{9,5},{10,6},{11,7},{12,8},{13,9},{1... | collective-permute-start | bytes 3080 | tf_op jit(solution)/shard_map/ppermute | solution.py:14
  108.5 9.5 %collective-permute-start.18 = (f32[2,4,4,8]{3,2,1,0:T(4,128)S(1)}, f32[2,4,4,8]{3,2,1,0:T(4,128)S(1)}, u32[]{:S(2)}, u32[]{:S(2)}) collective-permute-start(f32[2,4,4,8]{3,2,1,0:T(4,128)S(1)} %broadcast_select_fusion.4), channel_id=1, source_target_pairs={{8,0},{9,1},{10,2},{11,3},{12,4},{13,5},{14,6},{15,7},{16,8},{17,9... | collective-permute-start | bytes 3080 | tf_op jit(solution)/shard_map/ppermute | solution.py:14
  118.1 5.6 %collective-permute-start.19 = (f32[2,4,4,8]{3,2,1,0:T(4,128)S(1)}, f32[2,4,4,8]{3,2,1,0:T(4,128)S(1)}, u32[]{:S(2)}, u32[]{:S(2)}) collective-permute-start(f32[2,4,4,8]{3,2,1,0:T(4,128)S(1)} %broadcast_select_fusion.6), channel_id=1, source_target_pairs={{16,0},{17,1},{18,2},{19,3},{20,4},{21,5},{22,6},{23,7},{24,8},{25... | collective-permute-start | bytes 3080 | tf_op jit(solution)/shard_map/ppermute | solution.py:14
  123.8 33.4 %collective-permute-start.20 = (f32[2,4,4,8]{3,2,1,0:T(4,128)S(1)}, f32[2,4,4,8]{3,2,1,0:T(4,128)S(1)}, u32[]{:S(2)}, u32[]{:S(2)}) collective-permute-start(f32[2,4,4,8]{3,2,1,0:T(4,128)S(1)} %broadcast_select_fusion.8), channel_id=1, source_target_pairs={{32,0},{33,1},{34,2},{35,3},{36,4},{37,5},{38,6},{39,7},{40,8},{41... | collective-permute-start | bytes 3080 | tf_op jit(solution)/shard_map/ppermute | solution.py:14
  127.3 47.5 %collective-permute-start.11 = (f32[4,1,8,2048]{3,2,1,0:T(8,128)}, f32[4,1,8,2048]{3,2,1,0:T(8,128)}, u32[]{:S(2)}, u32[]{:S(2)}) collective-permute-start(f32[4,1,8,2048]{3,2,1,0:T(8,128)} %get-tuple-element.19), channel_id=1, source_target_pairs={{64,0},{128,64},{192,128},{256,192},{320,256},{384,320},{448,384},... | collective-permute-start | bytes 786440 | tf_op jit(solution)/shard_map/ppermute | solution.py:27
  129.3 45.6 %collective-permute-start.12 = (f32[4,1,8,2048]{3,2,1,0:T(8,128)}, f32[4,1,8,2048]{3,2,1,0:T(8,128)}, u32[]{:S(2)}, u32[]{:S(2)}) collective-permute-start(f32[4,1,8,2048]{3,2,1,0:T(8,128)} %get-tuple-element.18), channel_id=1, source_target_pairs={{0,64},{64,128},{128,192},{192,256},{256,320},{320,384},{384,448},... | collective-permute-start | bytes 786440 | tf_op jit(solution)/shard_map/ppermute | solution.py:25
  139.9 32.8 %collective-permute-start.13 = (f32[4,4,1,2048]{3,1,2,0:T(4,128)}, f32[4,4,1,2048]{3,1,2,0:T(4,128)}, u32[]{:S(2)}, u32[]{:S(2)}) collective-permute-start(f32[4,4,1,2048]{3,1,2,0:T(4,128)} %copy.43), channel_id=1, source_target_pairs={{1,0},{2,1},{3,2},{4,3},{5,4},{6,5},{7,6},{8,7},{9,8},{10,9},{11,1... | collective-permute-start | bytes 393224 | tf_op jit(solution)/shard_map/ppermute | solution.py:27
  155.3 18.5 %collective-permute-start.14 = (f32[4,4,1,2048]{3,1,2,0:T(4,128)}, f32[4,4,1,2048]{3,1,2,0:T(4,128)}, u32[]{:S(2)}, u32[]{:S(2)}) collective-permute-start(f32[4,4,1,2048]{3,1,2,0:T(4,128)} %copy.45), channel_id=1, source_target_pairs={{0,1},{1,2},{2,3},{3,4},{4,5},{5,6},{6,7},{7,8},{8,9},{9,10},{10,1... | collective-permute-start | bytes 393224 | tf_op jit(solution)/shard_map/ppermute | solution.py:25
  157.3 9.0 %collective-permute-start.21 = (f32[2,4,4,8]{3,2,1,0:T(4,128)S(1)}, f32[2,4,4,8]{3,2,1,0:T(4,128)S(1)}, u32[]{:S(2)}, u32[]{:S(2)}) collective-permute-start(f32[2,4,4,8]{3,2,1,0:T(4,128)S(1)} %broadcast_select_fusion.10), channel_id=1, source_target_pairs={{1,0},{2,1},{3,2},{4,3},{5,4},{6,5},{7,6},{8,7},{9,8},{10,9},{11,1... | collective-permute-start | bytes 3080 | tf_op jit(solution)/shard_map/ppermute | solution.py:14
  176.3 1.0 copy-start.6
  176.3 1.0 copy-start.7
  176.5 1.3 copy-start.3
where the time goes:
time: 182 us; the launch traced here: 181 us
  starting transfers between devices  104 us (57%)
  waiting for transfers between devices  31.5 us (17%)
  local copies, waits for them, and re-layouts  26.5 us (15%)
  other arithmetic  13.8 us (8%)
  between operations  5.59 us (3%)
    ppermute x14, starting transfers between devices, from_behind(): return lax.ppermute(block, axis, route)  57.7 us
    ppermute x14, waiting for transfers between devices, from_behind(): return lax.ppermute(block, axis, route)  31.5 us
    ppermute x4, starting transfers between devices, with_halo(): lax.ppermute(tail, axis, [(i, (i + 1) % count) for i in range(ends)])  23 us
    ppermute x4, starting transfers between devices, with_halo(): lax.ppermute(head, axis, [((i + 1) % count, i) for i in range(ends)])  22.8 us
    unnamed x26, local copies, waits for them, and re-layouts  4.58 us
    slice x5, local copies, waits for them, and re-layouts, with_halo(): lax.slice_in_dim(cells, cells.shape[dim] - width, cells.shape[dim], axis=...  3.73 us
  transfers between devices with their start and end apart: 22, of which 10 were waited for; matrix products, arithmetic and copies ran while one was open for 15% of the time, Pallas kernels for 0%

commit v1 on v0

v1 whole, which is shorter than its diff:
```python
import functools

import jax
import jax.numpy as jnp
from jax import lax
from jax.experimental import pallas as pl
from jax.experimental.pallas import tpu as pltpu
from jax.sharding import PartitionSpec as P

DT = 0.2
NU = 0.05
EDDY = 0.05
LANE = 128
ROWS = 8
CHUNK = 256

f32 = jnp.float32


def iota(shape, dim):
    return lax.broadcasted_iota(jnp.int32, shape, dim)


def vmem():
    return pl.BlockSpec(memory_space=pltpu.VMEM)


def smem():
    return pl.BlockSpec(memory_space=pltpu.SMEM)


def hbm():
    return pl.BlockSpec(memory_space=pl.ANY)


def shape(*dims):
    return jax.ShapeDtypeStruct(dims, f32)


def params(mib=48):
    return pltpu.CompilerParams(vmem_limit_bytes=mib << 20)


def cross_kernel(start_ref, state, out, sem):
    copy = pltpu.make_async_copy(state.at[:, pl.ds(start_ref[0], 2)], out, sem)
    copy.start()
    copy.wait()


def pack_kernel(state, up_msg, dn_msg, low, high, st, sems):
    load = pltpu.make_async_copy(state, st, sems.at[0])
    load.start()
    load.wait()
    copy_low = pltpu.make_async_copy(st.at[:, 0:2], low, sems.at[1])
    copy_high = pltpu.make_async_copy(st.at[:, 2:4], high, sems.at[2])
    copy_low.start()
    copy_high.start()
    comps, planes, cells, radial = st.shape
    inner = radial // 2
    for c in range(comps):
        for p in range(planes):
            up_msg[c, p : p + 1, :] = st[c, p, cells - 1 : cells, :]
            up_msg[c, planes + p : planes + p + 1, :] = st[c, p, cells - 2 : cells - 1, :]
            dn_msg[c, p : p + 1, :] = st[c, p, 0:1, :]
            dn_msg[c, planes + p : planes + p + 1, :] = st[c, p, 1:2, :]
    lane = iota((ROWS, LANE), 1)
    zero = jnp.zeros((ROWS, radial - comps * LANE), f32)
    up_msg[comps, :, comps * LANE :] = zero
    dn_msg[comps, :, comps * LANE :] = zero
    for c in range(comps):
        tile = jnp.zeros((ROWS, LANE), f32)
        for p in range(planes):
            below = st[c, p, :, inner - LANE : inner]
            above = st[c, p, :, inner : inner + LANE]
            for layer, (source, at) in enumerate(((below, LANE - 2), (below, LANE - 1), (above, 0), (above, 1))):
                to = layer * 8 + p + 1
                tile = jnp.where(lane == to, pltpu.roll(source, (to - at) % LANE, 1), tile)
        up_msg[comps, :, c * LANE : (c + 1) * LANE] = tile
        dn_msg[comps, :, c * LANE : (c + 1) * LANE] = tile
    copy_low.wait()
    copy_high.wait()


def window_kernel(turn_ref, s_raw, w_raw, left, right, to_next, to_prev, s_win, w_win):
    comps = s_win.shape[0]
    planes = 4
    turn = turn_ref[0]
    radial = left.shape[2]
    lane = iota((2 * ROWS, LANE), 1)
    zero = jnp.zeros((ROWS, LANE), f32)

    def window(raw, c, start):
        cells = [raw[:, (k * comps + c) * LANE : (k * comps + c + 1) * LANE] for k in range(3)]
        whole = jnp.concatenate(cells + [zero], axis=0)
        return pltpu.roll(whole, 4 * ROWS - start, 0)[: 2 * ROWS]

    for c in range(comps):
        sw = window(s_raw, c, 7 + turn)
        ww = window(w_raw, c, 6 - turn)
        s_win[c] = sw
        w_win[c] = ww
        both = jnp.where(lane >= 16, sw, ww)
        for k in range(2):
            at = radial + (2 * c + k) * LANE
            to_next[:, at : at + LANE] = both[k * ROWS : (k + 1) * ROWS]
            to_prev[:, at : at + LANE] = both[k * ROWS : (k + 1) * ROWS]
        to_next[2 * c : 2 * c + 1, :radial] = left[c, planes - 1 : planes, :]
        to_next[2 * c + 1 : 2 * c + 2, :radial] = right[c, planes - 1 : planes, :]
        to_prev[2 * c : 2 * c + 1, :radial] = left[c, 0:1, :]
        to_prev[2 * c + 1 : 2 * c + 2, :radial] = right[c, 0:1, :]


def advance(q, up_p, dn_p, up_t, dn_t, up_r, dn_r):
    n = len(q)
    gp = [up_p[c] - dn_p[c] for c in range(n)]
    gt = [up_t[c] - dn_t[c] for c in range(n)]
    gr = [up_r[c] - dn_r[c] for c in range(n)]
    strain = gp[0] * gp[0] + gt[0] * gt[0] + gr[0] * gr[0]
    for c in (1, 2):
        strain = strain + (gp[c] * gp[c] + gt[c] * gt[c] + gr[c] * gr[c])
    visc = DT * NU + (DT * EDDY) * jnp.sqrt(0.25 * strain)
    v = [(0.5 * DT) * q[c] for c in range(3)]
    result = []
    for c in range(n):
        second = (up_p[c] + dn_p[c]) + (up_t[c] + dn_t[c]) + (up_r[c] + dn_r[c]) - 6.0 * q[c]
        carried = v[0] * gp[c] + v[1] * gt[c] + v[2] * gr[c]
        result.append(q[c] + (visc * second - carried))
    return result


def step_kernel(
    info, frac, state, crossed, from_prev, from_next,
    left, right, up_msg, dn_msg, low_edge, high_edge, s_win, w_win, own,
    out,
    field, sect, edge, edge_sect, ghost1, ghost2, result, sems,
):
    comps, planes, cells, radial = result.shape
    inner = radial // 2
    position, last, half = info[0], info[1], info[2]
    f = frac[0]
    body = slice(LANE, LANE + radial)
    get_state = pltpu.make_async_copy(state, field.at[:, 2 : 2 + planes, :, body], sems.at[0])
    get_state.start()
    low_dst = field.at[:, 0:2, :, body]
    high_dst = field.at[:, 2 + planes : 4 + planes, :, body]

    @pl.when(position == half)
    def _():
        pltpu.make_async_copy(crossed, low_dst, sems.at[1]).start()

    @pl.when(position != half)
    def _():
        pltpu.make_async_copy(from_prev, low_dst, sems.at[1]).start()

    @pl.when(position == half - 1)
    def _():
        pltpu.make_async_copy(crossed, high_dst, sems.at[2]).start()

    @pl.when(position != half - 1)
    def _():
        pltpu.make_async_copy(from_next, high_dst, sems.at[2]).start()

    for ref in (field, sect):
        side = jnp.zeros(ref.shape[:3] + (LANE,), f32)
        ref[:, :, :, 0:LANE] = side
        ref[:, :, :, LANE + radial :] = side
    for ref in (edge, edge_sect):
        side = jnp.zeros(ref.shape[:2] + (LANE,), f32)
        ref[:, :, 0:LANE] = side
        ref[:, :, LANE + radial :] = side

    lane = iota((2 * ROWS, LANE), 1)
    lane8 = iota((ROWS, LANE), 1)
    row8 = iota((ROWS, LANE), 0)

    def lanes(x, by):
        return pltpu.roll(x, by % LANE, 1)

    def rows(x, by):
        return pltpu.roll(x, by % x.shape[0], 0)

    s2, s3, w1, w0, own_s, own_w = [], [], [], [], [], []
    for c in range(comps):
        at = [radial + (2 * c + k) * LANE for k in range(2)]
        low = jnp.concatenate([low_edge[:, a : a + LANE] for a in at], axis=0)
        high = jnp.concatenate([high_edge[:, a : a + LANE] for a in at], axis=0)
        low, high = lanes(low, -planes), lanes(high, planes)
        is_low, is_high = lane % 8 == 0, lane % 8 == planes + 1
        sw = jnp.where(is_low, low, jnp.where(is_high, high, s_win[c]))
        ww = jnp.where(is_low, low, jnp.where(is_high, high, w_win[c]))
        s2.append(lanes(sw, -16))
        s3.append(lanes(sw, -24))
        w1.append(lanes(ww, -8))
        w0.append(ww)
        mine = [own[:, (k * comps + c) * LANE : (k * comps + c + 1) * LANE] for k in range(3)]
        mine = jnp.concatenate(mine + [jnp.zeros((ROWS, LANE), f32)], axis=0)
        own_s.append(lanes(mine, -16))
        own_w.append(lanes(mine, -8))

    def blend_rot(x):
        return (1.0 - f) * x + f * rows(x, -1)

    def blend_sta(x):
        return f * x + (1.0 - f) * rows(x, -1)

    for kind, layer, blend in ((0, s2, blend_rot), (1, w1, blend_sta)):
        for c in range(comps):
            g = blend(layer[c])
            here = rows(g, -1)[:ROWS]
            for s in range(planes + 2):
                ghost1[kind, s, c] = jnp.broadcast_to(here[:, s : s + 1], (ROWS, LANE))
            first = jnp.broadcast_to(g[0:1, :], (ROWS, LANE))
            after = jnp.broadcast_to(g[cells + 1 : cells + 2, :], (ROWS, LANE))
            picked = jnp.where(row8 < planes, first, after)
            picked = jnp.where(lane8 == row8 % planes + 1, picked, 0.0)
            ghost1[kind, planes + 2, c] = jnp.broadcast_to(jnp.sum(picked, axis=1, keepdims=True), (ROWS, LANE))

    def far_section(q, up_r, dn_r):
        return advance(
            q,
            [lanes(x, -1) for x in q], [lanes(x, 1) for x in q],
            [rows(x, -1) for x in q], [rows(x, 1) for x in q],
            up_r, dn_r,
        )

    far_sta = [rows(blend_sta(x), -6)[: 2 * ROWS] for x in own_w]
    far_rot = [rows(blend_rot(x), -6)[: 2 * ROWS] for x in own_s]
    sec_s = far_section(s2, s3, far_sta)
    sec_w = far_section(w1, far_rot, w0)
    for kind, layer, blend in ((0, sec_s, blend_rot), (1, sec_w, blend_sta)):
        for c in range(comps):
            here = rows(blend(layer[c]), -1)[:ROWS]
            for p in range(planes):
                ghost2[kind, p, c] = jnp.broadcast_to(here[:, p + 1 : p + 2], (ROWS, LANE))

    row = iota((ROWS, CHUNK), 0)
    column = iota((ROWS, CHUNK), 1)
    wide = CHUNK // LANE

    def radial_pair(load, rot, sta, base):
        ahead = load(base + LANE, CHUNK + LANE)
        behind = load(base, CHUNK + LANE)
        up = pltpu.roll(ahead, CHUNK + LANE - 1, 1)[:, :CHUNK]
        dn = pltpu.roll(behind, 1, 1)[:, LANE:]
        up = jnp.where(column == inner - 1 - base, jnp.concatenate([rot] * wide, 1), up)
        dn = jnp.where(column == inner - base, jnp.concatenate([sta] * wide, 1), dn)
        return up, dn

    def azimuthal_pair(q, before, after):
        up = jnp.where(row == cells - 1, after, pltpu.roll(q, ROWS - 1, 0))
        dn = jnp.where(row == 0, before, pltpu.roll(q, 1, 0))
        return up, dn

    def span(base, width):
        return pl.ds(pl.multiple_of(base, LANE), width)

    get_state.wait()
    pltpu.make_async_copy(from_prev, low_dst, sems.at[1]).wait()
    pltpu.make_async_copy(from_next, high_dst, sems.at[2]).wait()

    def build_edge(k, carry):
        base = k * CHUNK
        at = span(base, CHUNK)
        for c in range(comps):
            tile = jnp.where(row < planes, left[c, :, at], pltpu.roll(right[c, :, at], planes, 0))
            edge[c, :, span(base + LANE, CHUNK)] = tile
        return carry

    lax.fori_loop(0, radial // CHUNK, build_edge, 0)

    def first(k, carry):
        base = k * CHUNK
        at, padded = span(base, CHUNK), span(base + LANE, CHUNK)
        for s in range(planes + 2):
            q, up_p, dn_p, up_t, dn_t, up_r, dn_r = [], [], [], [], [], [], []
            for c in range(comps):
                x = field[c, s + 1, :, padded]
                q.append(x)
                up_p.append(field[c, s + 2, :, padded])
                dn_p.append(field[c, s, :, padded])
                if s == 0:
                    before, after = low_edge[2 * c : 2 * c + 1, at], low_edge[2 * c + 1 : 2 * c + 2, at]
                elif s == planes + 1:
                    before, after = high_edge[2 * c : 2 * c + 1, at], high_edge[2 * c + 1 : 2 * c + 2, at]
                else:
                    before, after = left[c, s - 1 : s, at], right[c, s - 1 : s, at]
                u, d = azimuthal_pair(x, before, after)
                up_t.append(u)
                dn_t.append(d)
                u, d = radial_pair(
                    lambda b, w: field[c, s + 1, :, span(b, w)], ghost1[0, s, c], ghost1[1, s, c], base
                )
                up_r.append(u)
                dn_r.append(d)
            new = advance(q, up_p, dn_p, up_t, dn_t, up_r, dn_r)
            for c in range(comps):
                value = new[c]
                if s == 0:
                    value = jnp.where(position == 0, 0.0, value)
                elif s == planes + 1:
                    value = jnp.where(position == last, 0.0, value)
                sect[c, s, :, padded] = value
        q, up_p, dn_p, up_t, dn_t, up_r, dn_r = [], [], [], [], [], [], []
        for c in range(comps):
            x = edge[c, :, padded]
            q.append(x)
            u, d = pltpu.roll(x, ROWS - 1, 0), pltpu.roll(x, 1, 0)
            u = jnp.where(row == planes - 1, high_edge[2 * c : 2 * c + 1, at], u)
            u = jnp.where(row == 2 * planes - 1, high_edge[2 * c + 1 : 2 * c + 2, at], u)
            d = jnp.where(row == 0, low_edge[2 * c : 2 * c + 1, at], d)
            d = jnp.where(row == planes, low_edge[2 * c + 1 : 2 * c + 2, at], d)
            up_p.append(u)
            dn_p.append(d)
            up_t.append(jnp.where(row < planes, dn_msg[c, :, at], right[c, :, at]))
            dn_t.append(pltpu.roll(jnp.where(row < planes, up_msg[c, :, at], left[c, :, at]), planes, 0))
            u, d = radial_pair(
                lambda b, w: edge[c, :, span(b, w)], ghost1[0, planes + 2, c], ghost1[1, planes + 2, c], base
            )
            up_r.append(u)
            dn_r.append(d)
        new = advance(q, up_p, dn_p, up_t, dn_t, up_r, dn_r)
        for c in range(comps):
            edge_sect[c, :, at] = new[c]
        return carry

    lax.fori_loop(0, radial // CHUNK, first, 0)

    def second(k, carry):
        base = k * CHUNK
        at, padded = span(base, CHUNK), span(base + LANE, CHUNK)
        for p in range(planes):
            q, up_p, dn_p, up_t, dn_t, up_r, dn_r = [], [], [], [], [], [], []
            for c in range(comps):
                x = sect[c, p + 1, :, padded]
                q.append(x)
                up_p.append(sect[c, p + 2, :, padded])
                dn_p.append(sect[c, p, :, padded])
                u, d = azimuthal_pair(x, edge_sect[c, p : p + 1, at], edge_sect[c, planes + p : planes + p + 1, at])
                up_t.append(u)
                dn_t.append(d)
                u, d = radial_pair(
                    lambda b, w: sect[c, p + 1, :, span(b, w)], ghost2[0, p, c], ghost2[1, p, c], base
                )
                up_r.append(u)
                dn_r.append(d)
            new = advance(q, up_p, dn_p, up_t, dn_t, up_r, dn_r)
            for c in range(comps):
                result[c, p, :, at] = 0.5 * (field[c, p + 2, :, padded] + new[c])
        return carry

    lax.fori_loop(0, radial // CHUNK, second, 0)
    put = pltpu.make_async_copy(result, out, sems.at[3])
    put.start()
    put.wait()


def shards(state, rotor_offset, rotor_fraction):
    comps, planes, cells, radial = state.shape
    n_ax, n_az = lax.axis_size("ax"), lax.axis_size("az")
    half = n_ax // 2
    position = lax.axis_index("ax")
    offset = rotor_offset[0]
    shift = (offset + cells // 2) // cells
    turn = (offset - shift * cells)[None]
    info = jnp.stack([position, jnp.int32(n_ax - 1), jnp.int32(half)])
    two = (comps, 2, cells, radial)
    dma = pltpu.SemaphoreType.DMA

    bulk = pl.pallas_call(
        cross_kernel,
        out_shape=shape(*two),
        in_specs=[smem(), hbm()],
        out_specs=hbm(),
        scratch_shapes=[dma],
        name="pack_cross",
    )(jnp.where(position < half, planes - 2, 0)[None], state)
    crossed = lax.ppermute(bulk, "ax", [(half - 1, half), (half, half - 1)])

    up_msg, dn_msg, low, high = pl.pallas_call(
        pack_kernel,
        out_shape=[shape(comps + 1, cells, radial)] * 2 + [shape(*two)] * 2,
        in_specs=[hbm()],
        out_specs=[vmem(), vmem(), hbm(), hbm()],
        scratch_shapes=[pltpu.VMEM(state.shape, f32), dma((3,))],
        compiler_params=params(16),
        name="pack",
    )(state)
    left = lax.ppermute(up_msg, "az", [(i, (i + 1) % n_az) for i in range(n_az)])
    right = lax.ppermute(dn_msg, "az", [((i + 1) % n_az, i) for i in range(n_az)])
    plain = [i for i in range(n_ax - 1) if i != half - 1]
    from_prev = lax.ppermute(high, "ax", [(i, i + 1) for i in plain])
    from_next = lax.ppermute(low, "ax", [(i + 1, i) for i in plain])

    own = jnp.concatenate([m[comps, :, : comps * LANE] for m in (left, up_msg, right)], axis=1)
    total = cells * n_az
    lowest = (total // 4 + 8 + cells // 2) // cells
    highest = (3 * total // 4 - 9 + cells // 2) // cells

    def moved(block, by):
        ahead = lax.ppermute(block, "az", [((i + by) % n_az, i) for i in range(n_az)])
        back = lax.ppermute(block, "az", [(i, (i + by) % n_az) for i in range(n_az)])
        return ahead, back

    s_raw, w_raw = lax.switch(
        shift - lowest, [functools.partial(moved, by=by) for by in range(lowest, highest + 1)], own
    )
    to_next, to_prev, s_win, w_win = pl.pallas_call(
        window_kernel,
        out_shape=[shape(cells, radial + 2 * comps * LANE)] * 2 + [shape(comps, 2 * cells, LANE)] * 2,
        in_specs=[smem()] + [vmem()] * 4,
        out_specs=[vmem()] * 4,
        compiler_params=params(16),
        name="pack_window",
    )(turn, s_raw, w_raw, left, right)
    low_edge = lax.ppermute(to_next, "ax", [(i, i + 1) for i in range(n_ax - 1)])
    high_edge = lax.ppermute(to_prev, "ax", [(i + 1, i) for i in range(n_ax - 1)])

    wide = radial + 2 * LANE
    return pl.pallas_call(
        step_kernel,
        out_shape=shape(*state.shape),
        in_specs=[smem(), smem()] + [hbm()] * 4 + [vmem()] * 9,
        out_specs=hbm(),
        scratch_shapes=[
            pltpu.VMEM((comps, planes + 4, cells, wide), f32),
            pltpu.VMEM((comps, planes + 2, cells, wide), f32),
            pltpu.VMEM((comps, 2 * planes, wide), f32),
            pltpu.VMEM((comps, 2 * planes, wide), f32),
            pltpu.VMEM((2, planes + 3, comps, ROWS, LANE), f32),
            pltpu.VMEM((2, planes, comps, ROWS, LANE), f32),
            pltpu.VMEM(state.shape, f32),
            dma((4,)),
        ],
        compiler_params=params(),
        name="step",
    )(
        info, rotor_fraction, state, crossed, from_prev, from_next,
        left, right, up_msg, dn_msg, low_edge, high_edge, s_win, w_win, own,
    )


def solution(mesh):
    return jax.shard_map(
        shards,
        mesh=mesh,
        in_specs=(P(None, "ax", "az", None), P(), P()),
        out_specs=P(None, "ax", "az", None),
        check_vma=False,
    )
```

time: 182 us -> 100 us (0.55)
  starting transfers between devices: 104 us -> 49.7 us
  Pallas kernels: 0 us -> 27.1 us
  local copies, waits for them, and re-layouts: 26.5 us -> 2.75 us
  other arithmetic: 13.8 us -> 0.09 us
  waiting for transfers between devices: 31.5 us -> 18.1 us
  between operations: 5.59 us -> 1.46 us
    ppermute x22 -> x9, starting transfers between devices: 104 us -> 49.7 us  [the longest x1 18.5 us: shards(): lax.ppermute(dn_msg, 'az', [((i + 1) % n_az, i) for i in range(n_az)])]
    pallas_call x0 -> x4, Pallas kernels: none -> 27.1 us  [the longest x1 17 us: shards(): pl.pallas_call(cross_kernel, out_shape=shape(*two), in_specs=[smem(), hbm...]
    ppermute x22 -> x9, waiting for transfers between devices: 31.5 us -> 18.1 us  [the longest x1 8.05 us: shards(): lax.ppermute(to_prev, 'ax', [(i + 1, i) for i in range(n_ax - 1)])]
    slice x15 -> x0, local copies, waits for them, and re-layouts: 9.48 us -> none  [the longest x5 3.73 us: with_halo(): lax.slice_in_dim(cells, cells.shape[dim] - width, cells.shape[dim], axis=...]
    concatenate x4 -> x0, local copies, waits for them, and re-layouts: 6.35 us -> none  [the longest x2 3.4 us: radial_sides(): jnp.concatenate([field[..., 1:inner], ghost_rot[..., None], field[..., in...]
    mul x3 -> x0, other arithmetic: 4.88 us -> none  [the longest x1 3.12 us: shards(): 0.5 * (state + (section + step_size * evaluate(section, offset, fraction)))]
    sub x4 -> x0, other arithmetic: 4.43 us -> none  [the longest x2 2.98 us: tendency(): grad_t = (up_t - dn_t) * 0.5]
    ppermute x4 -> x0, local copies, waits for them, and re-layouts: 4.16 us -> none  [the longest x2 2.08 us: with_halo(): lax.ppermute(tail, axis, [(i, (i + 1) % count) for i in range(ends)])]
  transfers between devices with their start and end apart: 22 -> 9, of which waited for: 10 -> 5; matrix products, arithmetic and copies ran while one was open for 15% -> 1% of each run, Pallas kernels for 0% -> 18%
where the time goes in v1:
time: 100 us; the launch traced here: 99.2 us
  starting transfers between devices  49.7 us (50%)
  Pallas kernels  27.1 us (27%)
  waiting for transfers between devices  18.1 us (18%)
  local copies, waits for them, and re-layouts  2.75 us (3%)
  between operations  1.46 us (1%)
    ppermute x1, starting transfers between devices, shards(): lax.ppermute(dn_msg, 'az', [((i + 1) % n_az, i) for i in range(n_az)])  18.5 us
    pallas_call x1, Pallas kernels, shards(): pl.pallas_call(cross_kernel, out_shape=shape(*two), in_specs=[smem(), hbm...  17 us
    ppermute x1, starting transfers between devices, shards(): crossed = lax.ppermute(bulk, 'ax', [(half - 1, half), (half, half - 1)])  9.28 us
    ppermute x1, waiting for transfers between devices, shards(): lax.ppermute(to_prev, 'ax', [(i + 1, i) for i in range(n_ax - 1)])  8.05 us
    pallas_call x1, Pallas kernels, shards(): pl.pallas_call(step_kernel, out_shape=shape(*state.shape), in_specs=[smem...  7.41 us
    ppermute x1, waiting for transfers between devices, moved(): lax.ppermute(block, 'az', [((i + by) % n_az, i) for i in range(n_az)])  5.79 us
    ppermute x1, starting transfers between devices, shards(): from_next = lax.ppermute(low, 'ax', [(i + 1, i) for i in plain])  4.58 us
    ppermute x1, starting transfers between devices, moved(): lax.ppermute(block, 'az', [(i, (i + by) % n_az) for i in range(n_az)])  4.23 us
  transfers between devices with their start and end apart: 9, of which 5 were waited for; matrix products, arithmetic and copies ran while one was open for 1% of the time, Pallas kernels for 18%

profile of v1, /device:TPU:6, one launch (start us, length us, event | category | flops | bytes accessed | tf_op | source)
XLA Modules:
  0.0 99.2 jit_solution(3690874241593135793)
XLA Ops:
  0.0 0.0 copy-start
  0.0 1.2 %copy-done = f32[4,4,8,2048]{3,2,1,0:T(8,128)S(1)} copy-done((f32[4,4,8,2048]{3,2,1,0:T(8,128)S(1)}, f32[4,4,8,2048]{3,2,1,0:T(8,128)}, u32[]{:S(2)}) %copy-start) | copy-done | bytes 1048600
  1.2 1.8 %pack.1 = (f32[5,8,2048]{2,1,0:T(8,128)}, f32[5,8,2048]{2,1,0:T(8,128)}, f32[4,2,8,2048]{3,2,1,0:T(8,128)S(1)}, f32[4,2,8,2048]{3,2,1,0:T(8,128)}) custom-call(f32[4,4,8,2048]{3,2,1,0:T(8,128)S(1)} %copy-done), custom_call_target="tpu_custom_call" | custom-call | tf_op jit(solution)/shard_map/pack/pallas_call | solution.py:379
  3.1 0.0 copy-start.2
  3.1 0.8 copy-done.2
  3.9 18.5 %collective-permute-start.66 = (f32[5,8,2048]{2,1,0:T(8,128)}, f32[5,8,2048]{2,1,0:T(8,128)S(1)}, u32[]{:S(2)}, u32[]{:S(2)}) collective-permute-start(f32[5,8,2048]{2,1,0:T(8,128)} %get-tuple-element.49.dn_msg), channel_id=1, source_target_pairs={{1,0},{2,1},{3,2},{4,3},{5,4},{6,5},{7,6},{8,7},{9,8},{10,9},{11,1... | collective-permute-start | bytes 983048 | tf_op jit(solution)/shard_map/ppermute | solution.py:389
  22.4 0.0 copy-start.1
  22.4 17.0 %pack_cross.1 = f32[4,2,8,2048]{3,2,1,0:T(8,128)} custom-call(s32[1]{0:T(128)} %bitcast.1.start_ref, f32[4,4,8,2048]{3,2,1,0:T(8,128)} %state.5), custom_call_target="tpu_custom_call" | custom-call | tf_op jit(solution)/shard_map/pack_cross/pallas_call | solution.py:369
  39.4 9.3 %collective-permute-start.62 = (f32[4,2,8,2048]{3,2,1,0:T(8,128)}, f32[4,2,8,2048]{3,2,1,0:T(8,128)S(1)}, u32[]{:S(2)}, u32[]{:S(2)}) collective-permute-start(f32[4,2,8,2048]{3,2,1,0:T(8,128)} %pack_cross.1), channel_id=1, source_target_pairs={{192,256},{256,192},{193,257},{257,193},{194,258},{258,194},{195,2... | collective-permute-start | bytes 1572872 | tf_op jit(solution)/shard_map/ppermute | solution.py:377
  48.7 1.9 %collective-permute-start.65 = (f32[5,8,2048]{2,1,0:T(8,128)}, f32[5,8,2048]{2,1,0:T(8,128)S(1)}, u32[]{:S(2)}, u32[]{:S(2)}) collective-permute-start(f32[5,8,2048]{2,1,0:T(8,128)} %get-tuple-element.48.up_msg), channel_id=1, source_target_pairs={{0,1},{1,2},{2,3},{3,4},{4,5},{5,6},{6,7},{7,8},{8,9},{9,10},{10,1... | collective-permute-start | bytes 983048 | tf_op jit(solution)/shard_map/ppermute | solution.py:388
  50.6 1.3 %collective-permute-start.63 = (f32[4,2,8,2048]{3,2,1,0:T(8,128)}, f32[4,2,8,2048]{3,2,1,0:T(8,128)S(1)}, u32[]{:S(2)}, u32[]{:S(2)}) collective-permute-start(f32[4,2,8,2048]{3,2,1,0:T(8,128)} %get-tuple-element.46), channel_id=1, source_target_pairs={{0,64},{64,128},{128,192},{256,320},{320,384},{384,448},{1,65},{65... | collective-permute-start | bytes 1572872 | tf_op jit(solution)/shard_map/ppermute | solution.py:391
  51.9 4.6 %collective-permute-start.64 = (f32[4,2,8,2048]{3,2,1,0:T(8,128)}, f32[4,2,8,2048]{3,2,1,0:T(8,128)S(1)}, u32[]{:S(2)}, u32[]{:S(2)}) collective-permute-start(f32[4,2,8,2048]{3,2,1,0:T(8,128)} %copy-done.2), channel_id=1, source_target_pairs={{64,0},{128,64},{192,128},{320,256},{384,320},{448,384},{65,1},{12... | collective-permute-start | bytes 1572872 | tf_op jit(solution)/shard_map/ppermute | solution.py:392
  56.5 0.7 slice_bitcast_fusion.2
  58.6 0.0 collective-permute-done.66.right
  58.6 2.8 %collective-permute-done.65.left = f32[5,8,2048]{2,1,0:T(8,128)S(1)} collective-permute-done((f32[5,8,2048]{2,1,0:T(8,128)}, f32[5,8,2048]{2,1,0:T(8,128)S(1)}, u32[]{:S(2)}, u32[]{:S(2)}) %collective-permute-start.65) | collective-permute-done | bytes 327712 | tf_op jit(solution)/shard_map/ppermute | solution.py:388
  61.4 14.7 %conditional.1 = (f32[8,1536]{1,0:T(8,128)}, f32[8,1536]{1,0:T(8,128)}) conditional(s32[]{:T(128)} %clamp.3, f32[8,1536]{1,0:T(8,128)S(1)} %pad_maximum_fusion.own, f32[8,1536]{1,0:T(8,128)S(1)} %pad_maximum_fusion.own, f32[8,1536]{1,0:T(8,128)S(1)} %pad_maximum_fusion.own, ...), branch_computations={%region_0.1_spmd, %region_1.2_spmd, %region_2.3_spmd, %region_3.4_... | conditional | bytes 393312 | solution.py:404
  61.4 4.2 %collective-permute-start.21 = (f32[8,1536]{1,0:T(8,128)S(1)}, f32[8,1536]{1,0:T(8,128)}, u32[]{:S(2)}, u32[]{:S(2)}) collective-permute-start(f32[8,1536]{1,0:T(8,128)S(1)} %param.10), channel_id=1, source_target_pairs={{0,27},{1,28},{2,29},{3,30},{4,31},{5,32},{6,33},{7,34},{8,35},{9,... | collective-permute-start | bytes 147464 | tf_op jit(solution)/shard_map/cond/branch_10_fun/ppermute | solution.py:401
  65.7 4.0 %collective-permute-start.20 = (f32[8,1536]{1,0:T(8,128)S(1)}, f32[8,1536]{1,0:T(8,128)}, u32[]{:S(2)}, u32[]{:S(2)}) collective-permute-start(f32[8,1536]{1,0:T(8,128)S(1)} %param.10), channel_id=1, source_target_pairs={{27,0},{28,1},{29,2},{30,3},{31,4},{32,5},{33,6},{34,7},{35,8},{36... | collective-permute-start | bytes 147464 | tf_op jit(solution)/shard_map/cond/branch_10_fun/ppermute | solution.py:400
  69.7 0.7 collective-permute-done.21
  70.4 5.8 %collective-permute-done.20 = f32[8,1536]{1,0:T(8,128)} collective-permute-done((f32[8,1536]{1,0:T(8,128)S(1)}, f32[8,1536]{1,0:T(8,128)}, u32[]{:S(2)}, u32[]{:S(2)}) %collective-permute-start.20) | collective-permute-done | bytes 49184 | tf_op jit(solution)/shard_map/cond/branch_10_fun/ppermute | solution.py:400
  76.2 0.9 pack_window.1
  77.0 1.9 %collective-permute-start.67 = (f32[8,3072]{1,0:T(8,128)S(1)}, f32[8,3072]{1,0:T(8,128)S(1)}, u32[]{:S(2)}, u32[]{:S(2)}) collective-permute-start(f32[8,3072]{1,0:T(8,128)S(1)} %get-tuple-element.52), channel_id=1, source_target_pairs={{0,64},{64,128},{128,192},{192,256},{256,320},{320,384},{384,448},... | collective-permute-start | bytes 294920 | tf_op jit(solution)/shard_map/ppermute | solution.py:415
  79.0 3.9 %collective-permute-start.68 = (f32[8,3072]{1,0:T(8,128)S(1)}, f32[8,3072]{1,0:T(8,128)S(1)}, u32[]{:S(2)}, u32[]{:S(2)}) collective-permute-start(f32[8,3072]{1,0:T(8,128)S(1)} %get-tuple-element.53), channel_id=1, source_target_pairs={{64,0},{128,64},{192,128},{256,192},{320,256},{384,320},{448,384},... | collective-permute-start | bytes 294920 | tf_op jit(solution)/shard_map/ppermute | solution.py:416
  82.9 0.1 pad_add_fusion.info
  83.0 0.8 collective-permute-done.67.low_edge
  83.7 8.0 %collective-permute-done.68.high_edge = f32[8,3072]{1,0:T(8,128)S(1)} collective-permute-done((f32[8,3072]{1,0:T(8,128)S(1)}, f32[8,3072]{1,0:T(8,128)S(1)}, u32[]{:S(2)}, u32[]{:S(2)}) %collective-permute-start.68) | collective-permute-done | bytes 98336 | tf_op jit(solution)/shard_map/ppermute | solution.py:416
  91.8 0.0 collective-permute-done.62.crossed
  91.8 0.0 collective-permute-done.63.from_prev
  91.8 0.0 collective-permute-done.64.from_next
  91.8 0.0 copy-done.1
  91.8 7.4 %step.1 = f32[4,4,8,2048]{3,2,1,0:T(8,128)} custom-call(s32[3]{0:T(128)S(1)} %pad_add_fusion.info, f32[1]{0:T(128)S(6)} %copy.67.frac, f32[4,4,8,2048]{3,2,1,0:T(8,128)S(1)} %copy-done.1, f32[4,2,8,2048]{3,2,1,0:T(8,128)S(1)} %collective-permute-done.62.crossed, f32[4,2,8,2048]{3,2,1,0:T(8,128)S(1)} %collective-permute-done.63.from_prev, ...), custom_call_target="tpu_custom_call" | custom-call | tf_op jit(solution)/shard_map/step/pallas_call | solution.py:419
  (3 shorter events, 0.0 us)
Async XLA Ops:
  0.0 1.2 %copy-start = (f32[4,4,8,2048]{3,2,1,0:T(8,128)S(1)}, f32[4,4,8,2048]{3,2,1,0:T(8,128)}, u32[]{:S(2)}) copy-start(f32[4,4,8,2048]{3,2,1,0:T(8,128)} %state.5) | copy-start | bytes 3145732
  3.1 0.8 copy-start.2
  3.9 54.7 %collective-permute-start.66 = (f32[5,8,2048]{2,1,0:T(8,128)}, f32[5,8,2048]{2,1,0:T(8,128)S(1)}, u32[]{:S(2)}, u32[]{:S(2)}) collective-permute-start(f32[5,8,2048]{2,1,0:T(8,128)} %get-tuple-element.49.dn_msg), channel_id=1, source_target_pairs={{1,0},{2,1},{3,2},{4,3},{5,4},{6,5},{7,6},{8,7},{9,8},{10,9},{11,1... | collective-permute-start | bytes 983048 | tf_op jit(solution)/shard_map/ppermute | solution.py:389
  22.4 69.4 %copy-start.1 = (f32[4,4,8,2048]{3,2,1,0:T(8,128)S(1)}, f32[4,4,8,2048]{3,2,1,0:T(8,128)}, u32[]{:S(2)}) copy-start(f32[4,4,8,2048]{3,2,1,0:T(8,128)} %state.5) | copy-start | bytes 3145732
  39.4 52.4 %collective-permute-start.62 = (f32[4,2,8,2048]{3,2,1,0:T(8,128)}, f32[4,2,8,2048]{3,2,1,0:T(8,128)S(1)}, u32[]{:S(2)}, u32[]{:S(2)}) collective-permute-start(f32[4,2,8,2048]{3,2,1,0:T(8,128)} %pack_cross.1), channel_id=1, source_target_pairs={{192,256},{256,192},{193,257},{257,193},{194,258},{258,194},{195,2... | collective-permute-start | bytes 1572872 | tf_op jit(solution)/shard_map/ppermute | solution.py:377
  48.7 12.7 %collective-permute-start.65 = (f32[5,8,2048]{2,1,0:T(8,128)}, f32[5,8,2048]{2,1,0:T(8,128)S(1)}, u32[]{:S(2)}, u32[]{:S(2)}) collective-permute-start(f32[5,8,2048]{2,1,0:T(8,128)} %get-tuple-element.48.up_msg), channel_id=1, source_target_pairs={{0,1},{1,2},{2,3},{3,4},{4,5},{5,6},{6,7},{7,8},{8,9},{9,10},{10,1... | collective-permute-start | bytes 983048 | tf_op jit(solution)/shard_map/ppermute | solution.py:388
  50.6 41.2 %collective-permute-start.63 = (f32[4,2,8,2048]{3,2,1,0:T(8,128)}, f32[4,2,8,2048]{3,2,1,0:T(8,128)S(1)}, u32[]{:S(2)}, u32[]{:S(2)}) collective-permute-start(f32[4,2,8,2048]{3,2,1,0:T(8,128)} %get-tuple-element.46), channel_id=1, source_target_pairs={{0,64},{64,128},{128,192},{256,320},{320,384},{384,448},{1,65},{65... | collective-permute-start | bytes 1572872 | tf_op jit(solution)/shard_map/ppermute | solution.py:391
  51.9 39.9 %collective-permute-start.64 = (f32[4,2,8,2048]{3,2,1,0:T(8,128)}, f32[4,2,8,2048]{3,2,1,0:T(8,128)S(1)}, u32[]{:S(2)}, u32[]{:S(2)}) collective-permute-start(f32[4,2,8,2048]{3,2,1,0:T(8,128)} %copy-done.2), channel_id=1, source_target_pairs={{64,0},{128,64},{192,128},{320,256},{384,320},{448,384},{65,1},{12... | collective-permute-start | bytes 1572872 | tf_op jit(solution)/shard_map/ppermute | solution.py:392
  61.4 8.9 %collective-permute-start.21 = (f32[8,1536]{1,0:T(8,128)S(1)}, f32[8,1536]{1,0:T(8,128)}, u32[]{:S(2)}, u32[]{:S(2)}) collective-permute-start(f32[8,1536]{1,0:T(8,128)S(1)} %param.10), channel_id=1, source_target_pairs={{0,27},{1,28},{2,29},{3,30},{4,31},{5,32},{6,33},{7,34},{8,35},{9,... | collective-permute-start | bytes 147464 | tf_op jit(solution)/shard_map/cond/branch_10_fun/ppermute | solution.py:401
  65.7 10.5 %collective-permute-start.20 = (f32[8,1536]{1,0:T(8,128)S(1)}, f32[8,1536]{1,0:T(8,128)}, u32[]{:S(2)}, u32[]{:S(2)}) collective-permute-start(f32[8,1536]{1,0:T(8,128)S(1)} %param.10), channel_id=1, source_target_pairs={{27,0},{28,1},{29,2},{30,3},{31,4},{32,5},{33,6},{34,7},{35,8},{36... | collective-permute-start | bytes 147464 | tf_op jit(solution)/shard_map/cond/branch_10_fun/ppermute | solution.py:400
  77.0 6.7 %collective-permute-start.67 = (f32[8,3072]{1,0:T(8,128)S(1)}, f32[8,3072]{1,0:T(8,128)S(1)}, u32[]{:S(2)}, u32[]{:S(2)}) collective-permute-start(f32[8,3072]{1,0:T(8,128)S(1)} %get-tuple-element.52), channel_id=1, source_target_pairs={{0,64},{64,128},{128,192},{192,256},{256,320},{320,384},{384,448},... | collective-permute-start | bytes 294920 | tf_op jit(solution)/shard_map/ppermute | solution.py:415
  79.0 12.8 %collective-permute-start.68 = (f32[8,3072]{1,0:T(8,128)S(1)}, f32[8,3072]{1,0:T(8,128)S(1)}, u32[]{:S(2)}, u32[]{:S(2)}) collective-permute-start(f32[8,3072]{1,0:T(8,128)S(1)} %get-tuple-element.53), channel_id=1, source_target_pairs={{64,0},{128,64},{192,128},{256,192},{320,256},{384,320},{448,384},... | collective-permute-start | bytes 294920 | tf_op jit(solution)/shard_map/ppermute | solution.py:416

commit v2 on v1

v2 whole, which is shorter than its diff:
```python
import jax
import jax.numpy as jnp
from jax import lax
from jax.experimental import pallas as pl
from jax.experimental.pallas import tpu as pltpu
from jax.sharding import PartitionSpec as P

DT = 0.2
NU = 0.05
EDDY = 0.05
LANE = 128
ROWS = 8
CHUNK = 256

f32 = jnp.float32


def iota(shape, dim):
    return lax.broadcasted_iota(jnp.int32, shape, dim)


def vmem():
    return pl.BlockSpec(memory_space=pltpu.VMEM)


def smem():
    return pl.BlockSpec(memory_space=pltpu.SMEM)


def hbm():
    return pl.BlockSpec(memory_space=pl.ANY)


def shape(*dims):
    return jax.ShapeDtypeStruct(dims, f32)


def params(mib=48):
    return pltpu.CompilerParams(vmem_limit_bytes=mib << 20)


def pack_kernel(st, up_msg, dn_msg, low, high, layers):
    comps, planes, cells, radial = st.shape
    inner = radial // 2
    lane = iota((ROWS, LANE), 1)
    tile = jnp.zeros((ROWS, LANE), f32)
    for c in range(comps):
        for p in range(planes):
            up_msg[c, p : p + 1, :] = st[c, p, cells - 1 : cells, :]
            up_msg[c, planes + p : planes + p + 1, :] = st[c, p, cells - 2 : cells - 1, :]
            dn_msg[c, p : p + 1, :] = st[c, p, 0:1, :]
            dn_msg[c, planes + p : planes + p + 1, :] = st[c, p, 1:2, :]
            below = st[c, p, :, inner - LANE : inner]
            above = st[c, p, :, inner : inner + LANE]
            for layer, (source, at) in enumerate(((below, LANE - 2), (below, LANE - 1), (above, 0), (above, 1))):
                to = layer * 32 + c * 8 + p + 1
                tile = jnp.where(lane == to, pltpu.roll(source, (to - at) % LANE, 1), tile)
        for k in range(2):
            low[c, k] = st[c, k]
            high[c, k] = st[c, planes - 2 + k]
    layers[...] = tile


def window_kernel(where_ref, tiles, left, right, to_next, to_prev, s_win, w_win, own):
    comps = left.shape[0]
    planes = left.shape[1] // 2
    radial = left.shape[2]
    count = tiles.shape[0]
    sector, shift, turn = where_ref[0], where_ref[1], where_ref[2]

    def around(centre):
        found = [tiles[lax.rem(centre + (count + k), count)] for k in (-1, 0, 1)]
        return jnp.concatenate(found + [jnp.zeros((ROWS, LANE), f32)], axis=0)

    def window(centre, start):
        return pltpu.roll(around(centre), 4 * ROWS - start, 0)[: 2 * ROWS]

    sw = window(sector + shift, 7 + turn)
    ww = window(sector + count - shift, 6 - turn)
    s_win[...] = sw
    w_win[...] = ww
    own[...] = around(sector)
    both = jnp.where(iota((2 * ROWS, LANE), 1) >= 64, sw, ww)
    for msg, plane in ((to_next, planes - 1), (to_prev, 0)):
        for k in range(2):
            msg[:, radial + k * LANE : radial + (k + 1) * LANE] = both[k * ROWS : (k + 1) * ROWS]
        for c in range(comps):
            msg[2 * c : 2 * c + 1, :radial] = left[c, plane : plane + 1, :]
            msg[2 * c + 1 : 2 * c + 2, :radial] = right[c, plane : plane + 1, :]


def advance(q, up_p, dn_p, up_t, dn_t, up_r, dn_r):
    n = len(q)
    gp = [up_p[c] - dn_p[c] for c in range(n)]
    gt = [up_t[c] - dn_t[c] for c in range(n)]
    gr = [up_r[c] - dn_r[c] for c in range(n)]
    strain = gp[0] * gp[0] + gt[0] * gt[0] + gr[0] * gr[0]
    for c in (1, 2):
        strain = strain + (gp[c] * gp[c] + gt[c] * gt[c] + gr[c] * gr[c])
    visc = DT * NU + (DT * EDDY) * jnp.sqrt(0.25 * strain)
    v = [(0.5 * DT) * q[c] for c in range(3)]
    result = []
    for c in range(n):
        second = (up_p[c] + dn_p[c]) + (up_t[c] + dn_t[c]) + (up_r[c] + dn_r[c]) - 6.0 * q[c]
        carried = v[0] * gp[c] + v[1] * gt[c] + v[2] * gr[c]
        result.append(q[c] + (visc * second - carried))
    return result


def lanes(x, by):
    return pltpu.roll(x, by % LANE, 1)


def rows(x, by):
    return pltpu.roll(x, by % x.shape[0], 0)


def blend_rot(x, f):
    return (1.0 - f) * x + f * rows(x, -1)


def blend_sta(x, f):
    return f * x + (1.0 - f) * rows(x, -1)


def spread(x, at):
    return jnp.broadcast_to(x[:ROWS, at : at + 1], (ROWS, LANE))


def span(base, width):
    return pl.ds(pl.multiple_of(base, LANE), width)


def radial_pair(load, rot, sta, base, inner):
    column = iota((ROWS, CHUNK), 1)
    wide = CHUNK // LANE
    up = pltpu.roll(load(base + LANE, CHUNK + LANE), CHUNK + LANE - 1, 1)[:, :CHUNK]
    dn = pltpu.roll(load(base, CHUNK + LANE), 1, 1)[:, LANE:]
    up = jnp.where(column == inner - 1 - base, jnp.concatenate([rot] * wide, 1), up)
    dn = jnp.where(column == inner - base, jnp.concatenate([sta] * wide, 1), dn)
    return up, dn


def azimuthal_pair(q, before, after):
    row = iota(q.shape, 0)
    up = jnp.where(row == ROWS - 1, after, pltpu.roll(q, ROWS - 1, 0))
    dn = jnp.where(row == 0, before, pltpu.roll(q, 1, 0))
    return up, dn


def pad_zero(ref):
    side = jnp.zeros(ref.shape[:-1] + (LANE,), f32)
    ref[..., :LANE] = side
    ref[..., ref.shape[-1] - LANE :] = side


def own_kernel(frac, st, near_low, near_high, left, right, s_win, w_win, sect, field, ghost):
    comps, planes, cells, radial = st.shape
    inner = radial // 2
    f = frac[0]
    pad_zero(field)
    pad_zero(sect)
    for kind, win, at, blend in ((0, s_win, 64, blend_rot), (1, w_win, 32, blend_sta)):
        here = rows(blend(win[...], f), -1)
        for c in range(comps):
            for p in range(planes):
                ghost[kind, p, c] = spread(here, at + 8 * c + p + 1)

    def copy(k, carry):
        base = k * CHUNK
        for c in range(comps):
            for p in range(planes):
                field[c, p, :, span(base + LANE, CHUNK)] = st[c, p, :, span(base, CHUNK)]
        return carry

    lax.fori_loop(0, radial // CHUNK, copy, 0)

    def body(k, carry):
        base = k * CHUNK
        at, padded = span(base, CHUNK), span(base + LANE, CHUNK)
        for p in range(planes):
            q, up_p, dn_p, up_t, dn_t, up_r, dn_r = [], [], [], [], [], [], []
            for c in range(comps):
                x = st[c, p, :, at]
                q.append(x)
                up_p.append(near_high[c, 0, :, at] if p == planes - 1 else st[c, p + 1, :, at])
                dn_p.append(near_low[c, 1, :, at] if p == 0 else st[c, p - 1, :, at])
                u, d = azimuthal_pair(x, left[c, p : p + 1, at], right[c, p : p + 1, at])
                up_t.append(u)
                dn_t.append(d)
                u, d = radial_pair(
                    lambda b, w: field[c, p, :, span(b, w)], ghost[0, p, c], ghost[1, p, c], base, inner
                )
                up_r.append(u)
                dn_r.append(d)
            new = advance(q, up_p, dn_p, up_t, dn_t, up_r, dn_r)
            for c in range(comps):
                sect[c, p, :, padded] = new[c]
        return carry

    lax.fori_loop(0, radial // CHUNK, body, 0)


def step_kernel(
    info, frac, st, near_low, near_high, sect, left, right, up_msg, dn_msg, late_low, late_high, s_win, w_win, own,
    out,
    near, near_sect, edge, edge_sect, ghost1, ghost2, result, sem,
):
    comps, planes, cells, radial = st.shape
    inner = radial // 2
    position, last = info[0], info[1]
    f = frac[0]
    for ref in (near, near_sect, edge):
        pad_zero(ref)

    lane = iota((2 * ROWS, LANE), 1)
    lane8 = iota((ROWS, LANE), 1)
    row8 = iota((ROWS, LANE), 0)
    s2, s3, w1, w0, own_s, own_w = [], [], [], [], [], []
    is_low, is_high = lane % 8 == 0, lane % 8 == planes + 1
    at = [radial + k * LANE for k in range(2)]
    low = jnp.concatenate([late_low[:, a : a + LANE] for a in at], axis=0)
    high = jnp.concatenate([late_high[:, a : a + LANE] for a in at], axis=0)
    low, high = lanes(low, -planes), lanes(high, planes)
    sw = jnp.where(is_low, low, jnp.where(is_high, high, s_win[...]))
    ww = jnp.where(is_low, low, jnp.where(is_high, high, w_win[...]))
    mine = own[...]
    for c in range(comps):
        s2.append(lanes(sw, -64 - 8 * c))
        s3.append(lanes(sw, -96 - 8 * c))
        w1.append(lanes(ww, -32 - 8 * c))
        w0.append(lanes(ww, -8 * c))
        own_s.append(lanes(mine, -64 - 8 * c))
        own_w.append(lanes(mine, -32 - 8 * c))

    for kind, layer, blend in ((0, s2, blend_rot), (1, w1, blend_sta)):
        for c in range(comps):
            g = blend(layer[c], f)
            here = rows(g, -1)
            ghost1[kind, 0, c] = spread(here, 0)
            ghost1[kind, 1, c] = spread(here, planes + 1)
            first = jnp.broadcast_to(g[0:1, :], (ROWS, LANE))
            after = jnp.broadcast_to(g[cells + 1 : cells + 2, :], (ROWS, LANE))
            picked = jnp.where(row8 < planes, first, after)
            picked = jnp.where(lane8 == row8 % planes + 1, picked, 0.0)
            ghost1[kind, 2, c] = jnp.broadcast_to(jnp.sum(picked, axis=1, keepdims=True), (ROWS, LANE))

    def far_section(q, up_r, dn_r):
        return advance(
            q,
            [lanes(x, -1) for x in q], [lanes(x, 1) for x in q],
            [rows(x, -1) for x in q], [rows(x, 1) for x in q],
            up_r, dn_r,
        )

    far_sta = [rows(blend_sta(x, f), -6)[: 2 * ROWS] for x in own_w]
    far_rot = [rows(blend_rot(x, f), -6)[: 2 * ROWS] for x in own_s]
    sec_s = far_section(s2, s3, far_sta)
    sec_w = far_section(w1, far_rot, w0)
    for kind, layer, blend in ((0, sec_s, blend_rot), (1, sec_w, blend_sta)):
        for c in range(comps):
            here = rows(blend(layer[c], f), -1)
            for p in range(planes):
                ghost2[kind, p, c] = spread(here, p + 1)

    row = iota((ROWS, CHUNK), 0)

    def build(k, carry):
        base = k * CHUNK
        at, padded = span(base, CHUNK), span(base + LANE, CHUNK)
        for c in range(comps):
            edge[c, :, padded] = jnp.where(row < planes, left[c, :, at], pltpu.roll(right[c, :, at], planes, 0))
            near[c, 0, :, padded] = near_low[c, 1, :, at]
            near[c, 1, :, padded] = near_high[c, 0, :, at]
        return carry

    lax.fori_loop(0, radial // CHUNK, build, 0)

    def first(k, carry):
        base = k * CHUNK
        at, padded = span(base, CHUNK), span(base + LANE, CHUNK)
        for s, late, outside in ((0, late_low, 0), (1, late_high, last)):
            q, up_p, dn_p, up_t, dn_t, up_r, dn_r = [], [], [], [], [], [], []
            for c in range(comps):
                x = near[c, s, :, padded]
                q.append(x)
                far = near_high[c, 1, :, at] if s else near_low[c, 0, :, at]
                up_p.append(far if s else st[c, 0, :, at])
                dn_p.append(st[c, planes - 1, :, at] if s else far)
                u, d = azimuthal_pair(x, late[2 * c : 2 * c + 1, at], late[2 * c + 1 : 2 * c + 2, at])
                up_t.append(u)
                dn_t.append(d)
                u, d = radial_pair(
                    lambda b, w: near[c, s, :, span(b, w)], ghost1[0, s, c], ghost1[1, s, c], base, inner
                )
                up_r.append(u)
                dn_r.append(d)
            new = advance(q, up_p, dn_p, up_t, dn_t, up_r, dn_r)
            for c in range(comps):
                near_sect[c, s, :, padded] = jnp.where(position == outside, 0.0, new[c])
        q, up_p, dn_p, up_t, dn_t, up_r, dn_r = [], [], [], [], [], [], []
        for c in range(comps):
            x = edge[c, :, padded]
            q.append(x)
            u, d = pltpu.roll(x, ROWS - 1, 0), pltpu.roll(x, 1, 0)
            u = jnp.where(row == planes - 1, late_high[2 * c : 2 * c + 1, at], u)
            u = jnp.where(row == 2 * planes - 1, late_high[2 * c + 1 : 2 * c + 2, at], u)
            d = jnp.where(row == 0, late_low[2 * c : 2 * c + 1, at], d)
            d = jnp.where(row == planes, late_low[2 * c + 1 : 2 * c + 2, at], d)
            up_p.append(u)
            dn_p.append(d)
            up_t.append(jnp.where(row < planes, dn_msg[c, :, at], right[c, :, at]))
            dn_t.append(pltpu.roll(jnp.where(row < planes, up_msg[c, :, at], left[c, :, at]), planes, 0))
            u, d = radial_pair(
                lambda b, w: edge[c, :, span(b, w)], ghost1[0, 2, c], ghost1[1, 2, c], base, inner
            )
            up_r.append(u)
            dn_r.append(d)
        new = advance(q, up_p, dn_p, up_t, dn_t, up_r, dn_r)
        for c in range(comps):
            edge_sect[c, :, at] = new[c]
        return carry

    lax.fori_loop(0, radial // CHUNK, first, 0)

    def second(k, carry):
        base = k * CHUNK
        at, padded = span(base, CHUNK), span(base + LANE, CHUNK)
        for p in range(planes):
            q, up_p, dn_p, up_t, dn_t, up_r, dn_r = [], [], [], [], [], [], []
            for c in range(comps):
                x = sect[c, p, :, padded]
                q.append(x)
                up_p.append(near_sect[c, 1, :, padded] if p == planes - 1 else sect[c, p + 1, :, padded])
                dn_p.append(near_sect[c, 0, :, padded] if p == 0 else sect[c, p - 1, :, padded])
                u, d = azimuthal_pair(x, edge_sect[c, p : p + 1, at], edge_sect[c, planes + p : planes + p + 1, at])
                up_t.append(u)
                dn_t.append(d)
                u, d = radial_pair(
                    lambda b, w: sect[c, p, :, span(b, w)], ghost2[0, p, c], ghost2[1, p, c], base, inner
                )
                up_r.append(u)
                dn_r.append(d)
            new = advance(q, up_p, dn_p, up_t, dn_t, up_r, dn_r)
            for c in range(comps):
                result[c, p, :, at] = 0.5 * (st[c, p, :, at] + new[c])
        pltpu.make_async_copy(result.at[:, :, :, at], out.at[:, :, :, at], sem).start()
        return carry

    lax.fori_loop(0, radial // CHUNK, second, 0)
    pltpu.make_async_copy(result, out, sem).wait()


def shards(state, rotor_offset, rotor_fraction):
    comps, planes, cells, radial = state.shape
    n_ax, n_az = lax.axis_size("ax"), lax.axis_size("az")
    position = lax.axis_index("ax")
    offset = rotor_offset[0]
    shift = (offset + cells // 2) // cells
    turn = offset - shift * cells
    where = jnp.stack([lax.axis_index("az"), shift, turn])
    info = jnp.stack([position, jnp.int32(n_ax - 1)])

    up_msg, dn_msg, low, high, layers = pl.pallas_call(
        pack_kernel,
        out_shape=[shape(comps, cells, radial)] * 2 + [shape(comps, 2, cells, radial)] * 2 + [shape(ROWS, LANE)],
        in_specs=[vmem()],
        out_specs=[vmem()] * 5,
        compiler_params=params(16),
        name="pack",
    )(state)
    onward = [(i, i + 1) for i in range(n_ax - 1)]
    backward = [(i + 1, i) for i in range(n_ax - 1)]
    from_prev = lax.ppermute(high, "ax", onward)
    from_next = lax.ppermute(low, "ax", backward)
    left = lax.ppermute(up_msg, "az", [(i, (i + 1) % n_az) for i in range(n_az)])
    right = lax.ppermute(dn_msg, "az", [((i + 1) % n_az, i) for i in range(n_az)])

    tiles = lax.all_to_all(jnp.broadcast_to(layers, (n_az, ROWS, LANE)), "az", 0, 0)
    to_next, to_prev, s_win, w_win, own = pl.pallas_call(
        window_kernel,
        out_shape=[shape(cells, radial + 2 * LANE)] * 2 + [shape(2 * cells, LANE)] * 2 + [shape(4 * cells, LANE)],
        in_specs=[smem()] + [vmem()] * 3,
        out_specs=[vmem()] * 5,
        compiler_params=params(16),
        name="pack_window",
    )(where, tiles, left, right)
    late_low = lax.ppermute(to_next, "ax", onward)
    late_high = lax.ppermute(to_prev, "ax", backward)

    wide = radial + 2 * LANE
    cells_all = planes * cells * radial
    sect = pl.pallas_call(
        own_kernel,
        out_shape=shape(comps, planes, cells, wide),
        in_specs=[smem()] + [vmem()] * 7,
        out_specs=vmem(),
        scratch_shapes=[
            pltpu.VMEM((comps, planes, cells, wide), f32),
            pltpu.VMEM((2, planes, comps, ROWS, LANE), f32),
        ],
        cost_estimate=pl.CostEstimate(flops=120 * cells_all, bytes_accessed=48 * cells_all, transcendentals=cells_all),
        compiler_params=params(16),
        name="own_section",
    )(rotor_fraction, state, from_prev, from_next, left, right, s_win, w_win)
    return pl.pallas_call(
        step_kernel,
        out_shape=shape(*state.shape),
        in_specs=[smem(), smem()] + [vmem()] * 13,
        out_specs=hbm(),
        scratch_shapes=[
            pltpu.VMEM((comps, 2, cells, wide), f32),
            pltpu.VMEM((comps, 2, cells, wide), f32),
            pltpu.VMEM((comps, 2 * planes, wide), f32),
            pltpu.VMEM((comps, 2 * planes, radial), f32),
            pltpu.VMEM((2, 3, comps, ROWS, LANE), f32),
            pltpu.VMEM((2, planes, comps, ROWS, LANE), f32),
            pltpu.VMEM(state.shape, f32),
            pltpu.SemaphoreType.DMA,
        ],
        compiler_params=params(24),
        name="step",
    )(
        info, rotor_fraction, state, from_prev, from_next, sect,
        left, right, up_msg, dn_msg, late_low, late_high, s_win, w_win, own,
    )


def solution(mesh):
    return jax.shard_map(
        shards,
        mesh=mesh,
        in_specs=(P(None, "ax", "az", None), P(), P()),
        out_specs=P(None, "ax", "az", None),
        check_vma=False,
    )
```

time: 100 us -> 68.7 us (0.69)
  Pallas kernels: 27.1 us -> 8.57 us
  waiting for transfers between devices: 18.1 us -> 11 us
  starting transfers between devices: 49.7 us -> 45 us
    pallas_call x3, Pallas kernels: 19.7 us -> 3.6 us  [the longest x1 1.85 us: shards(): pl.pallas_call(own_kernel, out_shape=shape(comps, planes, cells, wide), i...]
    all_to_all x0 -> x1, starting transfers between devices: none -> 13.5 us  [shards(): lax.all_to_all(jnp.broadcast_to(layers, (n_az, ROWS, LANE)), 'az', 0, 0)]
    ppermute x1, starting transfers between devices: 18.5 us -> 7.55 us  [shards(): lax.ppermute(dn_msg, 'az', [((i + 1) % n_az, i) for i in range(n_az)])]
    ppermute x7 -> x4, starting transfers between devices: 29.3 us -> 22 us  [the longest x1 9.98 us: shards(): late_low = lax.ppermute(to_next, 'ax', onward)]
    ppermute x7 -> x4, waiting for transfers between devices: 15.3 us -> 8.49 us  [the longest x1 8.48 us: shards(): late_high = lax.ppermute(to_prev, 'ax', backward)]
    pallas_call x1, Pallas kernels: 7.41 us -> 4.97 us  [shards(): pl.pallas_call(step_kernel, out_shape=shape(*state.shape), in_specs=[smem...]
    ppermute x1, waiting for transfers between devices: 2.84 us -> 0.82 us  [shards(): lax.ppermute(up_msg, 'az', [(i, (i + 1) % n_az) for i in range(n_az)])]
    ppermute x1, waiting for transfers between devices: 0.01 us -> 1.65 us  [shards(): lax.ppermute(dn_msg, 'az', [((i + 1) % n_az, i) for i in range(n_az)])]
  transfers between devices with their start and end apart: 9 -> 7, of which waited for: 5 -> 3; matrix products, arithmetic and copies ran while one was open for 1% -> 0% of each run, Pallas kernels for 18% -> 4%
where the time goes in v2:
time: 68.7 us; the launch traced here: 68 us
  starting transfers between devices  45 us (66%)
  waiting for transfers between devices  11 us (16%)
  Pallas kernels  8.57 us (12%)
  local copies, waits for them, and re-layouts  1.95 us (3%)
  between operations  1.41 us (2%)
    all_to_all x1, starting transfers between devices, shards(): lax.all_to_all(jnp.broadcast_to(layers, (n_az, ROWS, LANE)), 'az', 0, 0)  13.5 us
    ppermute x1, starting transfers between devices, shards(): late_low = lax.ppermute(to_next, 'ax', onward)  9.98 us
    ppermute x1, waiting for transfers between devices, shards(): late_high = lax.ppermute(to_prev, 'ax', backward)  8.48 us
    ppermute x1, starting transfers between devices, shards(): from_prev = lax.ppermute(high, 'ax', onward)  8.13 us
    ppermute x1, starting transfers between devices, shards(): lax.ppermute(dn_msg, 'az', [((i + 1) % n_az, i) for i in range(n_az)])  7.55 us
    pallas_call x1, Pallas kernels, shards(): pl.pallas_call(step_kernel, out_shape=shape(*state.shape), in_specs=[smem...  4.97 us
    ppermute x1, starting transfers between devices, shards(): lax.ppermute(up_msg, 'az', [(i, (i + 1) % n_az) for i in range(n_az)])  1.92 us
    ppermute x1, starting transfers between devices, shards(): late_high = lax.ppermute(to_prev, 'ax', backward)  1.92 us
  transfers between devices with their start and end apart: 7, of which 3 were waited for; matrix products, arithmetic and copies ran while one was open for 0% of the time, Pallas kernels for 4%

profile of v2, /device:TPU:6, one launch (start us, length us, event | category | flops | bytes accessed | tf_op | source)
XLA Modules:
  0.0 68.0 jit_solution(16204924228384934311)
XLA Ops:
  0.0 0.0 copy-start
  0.0 1.2 %copy-done = f32[4,4,8,2048]{3,2,1,0:T(8,128)S(1)} copy-done((f32[4,4,8,2048]{3,2,1,0:T(8,128)S(1)}, f32[4,4,8,2048]{3,2,1,0:T(8,128)}, u32[]{:S(2)}) %copy-start) | copy-done | bytes 1048600
  1.2 0.0 copy-start.1
  1.2 1.2 %pack.1 = (f32[4,8,2048]{2,1,0:T(8,128)S(1)}, f32[4,8,2048]{2,1,0:T(8,128)S(1)}, f32[4,2,8,2048]{3,2,1,0:T(8,128)}, f32[4,2,8,2048]{3,2,1,0:T(8,128)}, f32[8,128]{1,0:T(8,128)S(1)}) custom-call(f32[4,4,8,2048]{3,2,1,0:T(8,128)S(1)} %copy-done), custom_call_target="tpu_custom_call" | custom-call | tf_op jit(solution)/shard_map/pack/pallas_call | solution.py:364
  2.4 0.7 %broadcast_in_dim.3 = f32[64,8,128]{2,1,0:T(8,128)} broadcast(f32[8,128]{1,0:T(8,128)S(1)} %get-tuple-element.19), dimensions={1,2} | broadcast | bytes 266240 | tf_op jit(solution)/shard_map/broadcast_in_dim | solution.py:379
  3.1 13.5 %all-to-all-start = ((f32[64,8,128]{2,1,0:T(8,128)}), f32[64,8,128]{2,1,0:T(8,128)S(1)}, u32[]{:S(2)}, u32[]{:S(2)}) async-start(f32[64,8,128]{2,1,0:T(8,128)} %broadcast_in_dim.3), calls=%async_computation | async-start | bytes 524288 | tf_op jit(solution)/shard_map/all_to_all | solution.py:379
  16.7 8.1 %collective-permute-start = (f32[4,2,8,2048]{3,2,1,0:T(8,128)}, f32[4,2,8,2048]{3,2,1,0:T(8,128)S(1)}, u32[]{:S(2)}, u32[]{:S(2)}) collective-permute-start(f32[4,2,8,2048]{3,2,1,0:T(8,128)} %get-tuple-element.15), channel_id=1, source_target_pairs={{0,64},{64,128},{128,192},{192,256},{256,320},{320,384},{384,448},... | collective-permute-start | bytes 1572872 | tf_op jit(solution)/shard_map/ppermute | solution.py:374
  24.8 1.9 %collective-permute-start.1 = (f32[4,2,8,2048]{3,2,1,0:T(8,128)}, f32[4,2,8,2048]{3,2,1,0:T(8,128)S(1)}, u32[]{:S(2)}, u32[]{:S(2)}) collective-permute-start(f32[4,2,8,2048]{3,2,1,0:T(8,128)} %get-tuple-element.16), channel_id=1, source_target_pairs={{64,0},{128,64},{192,128},{256,192},{320,256},{384,320},{448,384},... | collective-permute-start | bytes 1572872 | tf_op jit(solution)/shard_map/ppermute | solution.py:375
  26.7 1.9 %collective-permute-start.2 = (f32[4,8,2048]{2,1,0:T(8,128)S(1)}, f32[4,8,2048]{2,1,0:T(8,128)S(1)}, u32[]{:S(2)}, u32[]{:S(2)}) collective-permute-start(f32[4,8,2048]{2,1,0:T(8,128)S(1)} %get-tuple-element.17.up_msg), channel_id=1, source_target_pairs={{0,1},{1,2},{2,3},{3,4},{4,5},{5,6},{6,7},{7,8},{8,9},{9,10},{10,1... | collective-permute-start | bytes 786440 | tf_op jit(solution)/shard_map/ppermute | solution.py:376
  28.7 7.5 %collective-permute-start.3 = (f32[4,8,2048]{2,1,0:T(8,128)S(1)}, f32[4,8,2048]{2,1,0:T(8,128)S(1)}, u32[]{:S(2)}, u32[]{:S(2)}) collective-permute-start(f32[4,8,2048]{2,1,0:T(8,128)S(1)} %get-tuple-element.18.dn_msg), channel_id=1, source_target_pairs={{1,0},{2,1},{3,2},{4,3},{5,4},{6,5},{7,6},{8,7},{9,8},{10,9},{11,1... | collective-permute-start | bytes 786440 | tf_op jit(solution)/shard_map/ppermute | solution.py:377
  37.5 0.1 pad_add_fusion.1.where_ref
  37.6 0.8 %collective-permute-done.2.left = f32[4,8,2048]{2,1,0:T(8,128)S(1)} collective-permute-done((f32[4,8,2048]{2,1,0:T(8,128)S(1)}, f32[4,8,2048]{2,1,0:T(8,128)S(1)}, u32[]{:S(2)}, u32[]{:S(2)}) %collective-permute-start.2) | collective-permute-done | bytes 262176 | tf_op jit(solution)/shard_map/ppermute | solution.py:376
  38.4 1.7 %collective-permute-done.3.right = f32[4,8,2048]{2,1,0:T(8,128)S(1)} collective-permute-done((f32[4,8,2048]{2,1,0:T(8,128)S(1)}, f32[4,8,2048]{2,1,0:T(8,128)S(1)}, u32[]{:S(2)}, u32[]{:S(2)}) %collective-permute-start.3) | collective-permute-done | bytes 262176 | tf_op jit(solution)/shard_map/ppermute | solution.py:377
  40.1 0.0 all-to-all-done.tiles
  40.1 0.6 pack_window.1
  40.7 10.0 %collective-permute-start.4 = (f32[8,2304]{1,0:T(8,128)S(1)}, f32[8,2304]{1,0:T(8,128)S(1)}, u32[]{:S(2)}, u32[]{:S(2)}) collective-permute-start(f32[8,2304]{1,0:T(8,128)S(1)} %get-tuple-element.22), channel_id=1, source_target_pairs={{0,64},{64,128},{128,192},{192,256},{256,320},{320,384},{384,448},... | collective-permute-start | bytes 221192 | tf_op jit(solution)/shard_map/ppermute | solution.py:388
  50.7 1.9 %collective-permute-start.5 = (f32[8,2304]{1,0:T(8,128)S(1)}, f32[8,2304]{1,0:T(8,128)S(1)}, u32[]{:S(2)}, u32[]{:S(2)}) collective-permute-start(f32[8,2304]{1,0:T(8,128)S(1)} %get-tuple-element.23), channel_id=1, source_target_pairs={{64,0},{128,64},{192,128},{256,192},{320,256},{384,320},{448,384},... | collective-permute-start | bytes 221192 | tf_op jit(solution)/shard_map/ppermute | solution.py:389
  52.6 0.1 pad_add_fusion.info
  52.7 0.0 collective-permute-done.near_low
  52.7 0.0 collective-permute-done.1.near_high
  52.7 0.0 copy-done.1
  52.7 1.9 %own_section.1.sect = f32[4,4,8,2304]{3,2,1,0:T(8,128)S(1)} custom-call(f32[1]{0:T(128)S(6)} %copy.5.frac, f32[4,4,8,2048]{3,2,1,0:T(8,128)S(1)} %copy-done.1, f32[4,2,8,2048]{3,2,1,0:T(8,128)S(1)} %collective-permute-done.near_low, f32[4,2,8,2048]{3,2,1,0:T(8,128)S(1)} %collective-permute-done.1.near_high, f32[4,8,2048]{2,1,0:T(8,128)S(1)} %collective-permute-done.2.left, ...), custom_call_target="tpu_custom_call" | custom-call | flops 7864320 | bytes 3145728 | tf_op jit(solution)/shard_map/own_section/pallas_call | solution.py:393
  54.5 0.0 collective-permute-done.4.late_low
  54.6 8.5 %collective-permute-done.5.late_high = f32[8,2304]{1,0:T(8,128)S(1)} collective-permute-done((f32[8,2304]{1,0:T(8,128)S(1)}, f32[8,2304]{1,0:T(8,128)S(1)}, u32[]{:S(2)}, u32[]{:S(2)}) %collective-permute-start.5) | collective-permute-done | bytes 73760 | tf_op jit(solution)/shard_map/ppermute | solution.py:389
  63.0 5.0 %step.1 = f32[4,4,8,2048]{3,2,1,0:T(8,128)} custom-call(s32[2]{0:T(128)S(1)} %pad_add_fusion.info, f32[1]{0:T(128)S(6)} %copy.5.frac, f32[4,4,8,2048]{3,2,1,0:T(8,128)S(1)} %copy-done.1, f32[4,2,8,2048]{3,2,1,0:T(8,128)S(1)} %collective-permute-done.near_low, f32[4,2,8,2048]{3,2,1,0:T(8,128)S(1)} %collective-permute-done.1.near_high, ...), custom_call_target="tpu_custom_call" | custom-call | tf_op jit(solution)/shard_map/step/pallas_call | solution.py:406
Async XLA Ops:
  0.0 1.2 %copy-start = (f32[4,4,8,2048]{3,2,1,0:T(8,128)S(1)}, f32[4,4,8,2048]{3,2,1,0:T(8,128)}, u32[]{:S(2)}) copy-start(f32[4,4,8,2048]{3,2,1,0:T(8,128)} %st.5) | copy-start | bytes 3145732
  1.2 51.5 %copy-start.1 = (f32[4,4,8,2048]{3,2,1,0:T(8,128)S(1)}, f32[4,4,8,2048]{3,2,1,0:T(8,128)}, u32[]{:S(2)}) copy-start(f32[4,4,8,2048]{3,2,1,0:T(8,128)} %st.5) | copy-start | bytes 3145732
  3.1 37.0 %all-to-all-start = ((f32[64,8,128]{2,1,0:T(8,128)}), f32[64,8,128]{2,1,0:T(8,128)S(1)}, u32[]{:S(2)}, u32[]{:S(2)}) async-start(f32[64,8,128]{2,1,0:T(8,128)} %broadcast_in_dim.3), calls=%async_computation | async-start | bytes 524288 | tf_op jit(solution)/shard_map/all_to_all | solution.py:379
  16.7 36.0 %collective-permute-start = (f32[4,2,8,2048]{3,2,1,0:T(8,128)}, f32[4,2,8,2048]{3,2,1,0:T(8,128)S(1)}, u32[]{:S(2)}, u32[]{:S(2)}) collective-permute-start(f32[4,2,8,2048]{3,2,1,0:T(8,128)} %get-tuple-element.15), channel_id=1, source_target_pairs={{0,64},{64,128},{128,192},{192,256},{256,320},{320,384},{384,448},... | collective-permute-start | bytes 1572872 | tf_op jit(solution)/shard_map/ppermute | solution.py:374
  24.8 27.9 %collective-permute-start.1 = (f32[4,2,8,2048]{3,2,1,0:T(8,128)}, f32[4,2,8,2048]{3,2,1,0:T(8,128)S(1)}, u32[]{:S(2)}, u32[]{:S(2)}) collective-permute-start(f32[4,2,8,2048]{3,2,1,0:T(8,128)} %get-tuple-element.16), channel_id=1, source_target_pairs={{64,0},{128,64},{192,128},{256,192},{320,256},{384,320},{448,384},... | collective-permute-start | bytes 1572872 | tf_op jit(solution)/shard_map/ppermute | solution.py:375
  26.7 11.7 %collective-permute-start.2 = (f32[4,8,2048]{2,1,0:T(8,128)S(1)}, f32[4,8,2048]{2,1,0:T(8,128)S(1)}, u32[]{:S(2)}, u32[]{:S(2)}) collective-permute-start(f32[4,8,2048]{2,1,0:T(8,128)S(1)} %get-tuple-element.17.up_msg), channel_id=1, source_target_pairs={{0,1},{1,2},{2,3},{3,4},{4,5},{5,6},{6,7},{7,8},{8,9},{9,10},{10,1... | collective-permute-start | bytes 786440 | tf_op jit(solution)/shard_map/ppermute | solution.py:376
  28.7 11.4 %collective-permute-start.3 = (f32[4,8,2048]{2,1,0:T(8,128)S(1)}, f32[4,8,2048]{2,1,0:T(8,128)S(1)}, u32[]{:S(2)}, u32[]{:S(2)}) collective-permute-start(f32[4,8,2048]{2,1,0:T(8,128)S(1)} %get-tuple-element.18.dn_msg), channel_id=1, source_target_pairs={{1,0},{2,1},{3,2},{4,3},{5,4},{6,5},{7,6},{8,7},{9,8},{10,9},{11,1... | collective-permute-start | bytes 786440 | tf_op jit(solution)/shard_map/ppermute | solution.py:377
  40.7 13.9 %collective-permute-start.4 = (f32[8,2304]{1,0:T(8,128)S(1)}, f32[8,2304]{1,0:T(8,128)S(1)}, u32[]{:S(2)}, u32[]{:S(2)}) collective-permute-start(f32[8,2304]{1,0:T(8,128)S(1)} %get-tuple-element.22), channel_id=1, source_target_pairs={{0,64},{64,128},{128,192},{192,256},{256,320},{320,384},{384,448},... | collective-permute-start | bytes 221192 | tf_op jit(solution)/shard_map/ppermute | solution.py:388
  50.7 12.4 %collective-permute-start.5 = (f32[8,2304]{1,0:T(8,128)S(1)}, f32[8,2304]{1,0:T(8,128)S(1)}, u32[]{:S(2)}, u32[]{:S(2)}) collective-permute-start(f32[8,2304]{1,0:T(8,128)S(1)} %get-tuple-element.23), channel_id=1, source_target_pairs={{64,0},{128,64},{192,128},{256,192},{320,256},{384,320},{448,384},... | collective-permute-start | bytes 221192 | tf_op jit(solution)/shard_map/ppermute | solution.py:389

commit v3 on v2

--- a/solution.py
+++ b/solution.py
@@ -39,7 +39,15 @@
     return pltpu.CompilerParams(vmem_limit_bytes=mib << 20)
 
 
-def pack_kernel(st, up_msg, dn_msg, low, high, layers):
+def cross_kernel(info, st, crossing):
+    planes = st.shape[1]
+    below = info[0] < info[2]
+    for c in range(st.shape[0]):
+        for k in range(2):
+            crossing[c, k] = jnp.where(below, st[c, planes - 2 + k], st[c, k])
+
+
+def pack_kernel(st, crossing, up_msg, dn_msg, low, high, layers):
     comps, planes, cells, radial = st.shape
     inner = radial // 2
     lane = iota((ROWS, LANE), 1)
@@ -154,10 +162,15 @@
     ref[..., ref.shape[-1] - LANE :] = side
 
 
-def own_kernel(frac, st, near_low, near_high, left, right, s_win, w_win, sect, field, ghost):
+def choose(crossing, crossed, plain, c, k, at):
+    return jnp.where(crossing, crossed[c, k, :, at], plain[c, k, :, at])
+
+
+def own_kernel(info, frac, st, crossed, near_low, near_high, left, right, s_win, w_win, sect, field, ghost):
     comps, planes, cells, radial = st.shape
     inner = radial // 2
     f = frac[0]
+    from_below, from_above = info[0] == info[2], info[0] == info[2] - 1
     pad_zero(field)
     pad_zero(sect)
     for kind, win, at, blend in ((0, s_win, 64, blend_rot), (1, w_win, 32, blend_sta)):
@@ -183,8 +196,8 @@
             for c in range(comps):
                 x = st[c, p, :, at]
                 q.append(x)
-                up_p.append(near_high[c, 0, :, at] if p == planes - 1 else st[c, p + 1, :, at])
-                dn_p.append(near_low[c, 1, :, at] if p == 0 else st[c, p - 1, :, at])
+                up_p.append(choose(from_above, crossed, near_high, c, 0, at) if p == planes - 1 else st[c, p + 1, :, at])
+                dn_p.append(choose(from_below, crossed, near_low, c, 1, at) if p == 0 else st[c, p - 1, :, at])
                 u, d = azimuthal_pair(x, left[c, p : p + 1, at], right[c, p : p + 1, at])
                 up_t.append(u)
                 dn_t.append(d)
@@ -202,13 +215,14 @@
 
 
 def step_kernel(
-    info, frac, st, near_low, near_high, sect, left, right, up_msg, dn_msg, late_low, late_high, s_win, w_win, own,
+    info, frac, st, crossed, near_low, near_high, sect, left, right, up_msg, dn_msg, late_low, late_high, s_win, w_win, own,
     out,
     near, near_sect, edge, edge_sect, ghost1, ghost2, result, sem,
 ):
     comps, planes, cells, radial = st.shape
     inner = radial // 2
     position, last = info[0], info[1]
+    from_below, from_above = position == info[2], position == info[2] - 1
     f = frac[0]
     for ref in (near, near_sect, edge):
         pad_zero(ref)
@@ -270,8 +284,8 @@
         at, padded = span(base, CHUNK), span(base + LANE, CHUNK)
         for c in range(comps):
             edge[c, :, padded] = jnp.where(row < planes, left[c, :, at], pltpu.roll(right[c, :, at], planes, 0))
-            near[c, 0, :, padded] = near_low[c, 1, :, at]
-            near[c, 1, :, padded] = near_high[c, 0, :, at]
+            near[c, 0, :, padded] = choose(from_below, crossed, near_low, c, 1, at)
+            near[c, 1, :, padded] = choose(from_above, crossed, near_high, c, 0, at)
         return carry
 
     lax.fori_loop(0, radial // CHUNK, build, 0)
@@ -284,7 +298,10 @@
             for c in range(comps):
                 x = near[c, s, :, padded]
                 q.append(x)
-                far = near_high[c, 1, :, at] if s else near_low[c, 0, :, at]
+                if s:
+                    far = choose(from_above, crossed, near_high, c, 1, at)
+                else:
+                    far = choose(from_below, crossed, near_low, c, 0, at)
                 up_p.append(far if s else st[c, 0, :, at])
                 dn_p.append(st[c, planes - 1, :, at] if s else far)
                 u, d = azimuthal_pair(x, late[2 * c : 2 * c + 1, at], late[2 * c + 1 : 2 * c + 2, at])
@@ -359,20 +376,30 @@
     shift = (offset + cells // 2) // cells
     turn = offset - shift * cells
     where = jnp.stack([lax.axis_index("az"), shift, turn])
-    info = jnp.stack([position, jnp.int32(n_ax - 1)])
-
+    half = n_ax // 2
+    info = jnp.stack([position, jnp.int32(n_ax - 1), jnp.int32(half)])
+
+    crossing = pl.pallas_call(
+        cross_kernel,
+        out_shape=shape(comps, 2, cells, radial),
+        in_specs=[smem(), vmem()],
+        out_specs=vmem(),
+        compiler_params=params(16),
+        name="pack_cross",
+    )(info, state)
+    crossed = lax.ppermute(crossing, "ax", [(half - 1, half), (half, half - 1)])
     up_msg, dn_msg, low, high, layers = pl.pallas_call(
         pack_kernel,
         out_shape=[shape(comps, cells, radial)] * 2 + [shape(comps, 2, cells, radial)] * 2 + [shape(ROWS, LANE)],
-        in_specs=[vmem()],
+        in_specs=[vmem(), hbm()],
         out_specs=[vmem()] * 5,
         compiler_params=params(16),
         name="pack",
-    )(state)
+    )(state, crossing)
     onward = [(i, i + 1) for i in range(n_ax - 1)]
     backward = [(i + 1, i) for i in range(n_ax - 1)]
-    from_prev = lax.ppermute(high, "ax", onward)
-    from_next = lax.ppermute(low, "ax", backward)
+    from_prev = lax.ppermute(high, "ax", [pair for pair in onward if half - 1 not in pair or half not in pair])
+    from_next = lax.ppermute(low, "ax", [pair for pair in backward if half - 1 not in pair or half not in pair])
     left = lax.ppermute(up_msg, "az", [(i, (i + 1) % n_az) for i in range(n_az)])
     right = lax.ppermute(dn_msg, "az", [((i + 1) % n_az, i) for i in range(n_az)])
 
@@ -393,7 +420,7 @@
     sect = pl.pallas_call(
         own_kernel,
         out_shape=shape(comps, planes, cells, wide),
-        in_specs=[smem()] + [vmem()] * 7,
+        in_specs=[smem(), smem()] + [vmem()] * 8,
         out_specs=vmem(),
         scratch_shapes=[
             pltpu.VMEM((comps, planes, cells, wide), f32),
@@ -402,11 +429,11 @@
         cost_estimate=pl.CostEstimate(flops=120 * cells_all, bytes_accessed=48 * cells_all, transcendentals=cells_all),
         compiler_params=params(16),
         name="own_section",
-    )(rotor_fraction, state, from_prev, from_next, left, right, s_win, w_win)
+    )(info, rotor_fraction, state, crossed, from_prev, from_next, left, right, s_win, w_win)
     return pl.pallas_call(
         step_kernel,
         out_shape=shape(*state.shape),
-        in_specs=[smem(), smem()] + [vmem()] * 13,
+        in_specs=[smem(), smem()] + [vmem()] * 14,
         out_specs=hbm(),
         scratch_shapes=[
             pltpu.VMEM((comps, 2, cells, wide), f32),
@@ -421,7 +448,7 @@
         compiler_params=params(24),
         name="step",
     )(
-        info, rotor_fraction, state, from_prev, from_next, sect,
+        info, rotor_fraction, state, crossed, from_prev, from_next, sect,
         left, right, up_msg, dn_msg, late_low, late_high, s_win, w_win, own,
     )
 

time: 68.7 us -> 67.1 us (0.977)
  waiting for transfers between devices: 11 us -> 8.63 us
  Pallas kernels: 8.57 us -> 10.8 us
  starting transfers between devices: 45 us -> 42.9 us
  local copies, waits for them, and re-layouts: 1.95 us -> 2.8 us
    ppermute x1, starting transfers between devices: 9.98 us -> 1.92 us  [shards(): late_low = lax.ppermute(to_next, 'ax', onward)]
    ppermute x2 -> x3, starting transfers between devices: 10.1 us -> 14 us  [the longest x1 8.13 us: shards(): crossed = lax.ppermute(crossing, 'ax', [(half - 1, half), (half, half - 1)])]
    ppermute x1, waiting for transfers between devices: 8.48 us -> 5.19 us  [shards(): late_high = lax.ppermute(to_prev, 'ax', backward)]
    ppermute x1, starting transfers between devices: 1.92 us -> 3.92 us  [shards(): late_high = lax.ppermute(to_prev, 'ax', backward)]
    pallas_call x0 -> x1, Pallas kernels: none -> 1.39 us  [shards(): pl.pallas_call(cross_kernel, out_shape=shape(comps, 2, cells, radial), in...]
    ppermute x1, waiting for transfers between devices: 0.82 us -> 1.67 us  [shards(): lax.ppermute(up_msg, 'az', [(i, (i + 1) % n_az) for i in range(n_az)])]
    unnamed x4 -> x12, local copies, waits for them, and re-layouts: 1.23 us -> 2.03 us
  transfers between devices with their start and end apart: 7 -> 8, of which waited for: 3 -> 3; matrix products, arithmetic and copies ran while one was open for 0% -> 0% of each run, Pallas kernels for 4% -> 5%
where the time goes in v3:
time: 67.1 us; the launch traced here: 66.7 us
  starting transfers between devices  42.9 us (64%)
  Pallas kernels  10.8 us (16%)
  waiting for transfers between devices  8.63 us (13%)
  local copies, waits for them, and re-layouts  2.8 us (4%)
  between operations  1.46 us (2%)
    all_to_all x1, starting transfers between devices, shards(): lax.all_to_all(jnp.broadcast_to(layers, (n_az, ROWS, LANE)), 'az', 0, 0)  13.5 us
    ppermute x1, starting transfers between devices, shards(): crossed = lax.ppermute(crossing, 'ax', [(half - 1, half), (half, half - 1)])  8.13 us
    ppermute x1, starting transfers between devices, shards(): lax.ppermute(dn_msg, 'az', [((i + 1) % n_az, i) for i in range(n_az)])  7.55 us
    pallas_call x1, Pallas kernels, shards(): pl.pallas_call(step_kernel, out_shape=shape(*state.shape), in_specs=[smem...  5.45 us
    ppermute x1, waiting for transfers between devices, shards(): late_high = lax.ppermute(to_prev, 'ax', backward)  5.19 us
    ppermute x1, starting transfers between devices, shards(): lax.ppermute(low, 'ax', [pair for pair in backward if half - 1 not in pai...  4.58 us
    ppermute x1, starting transfers between devices, shards(): late_high = lax.ppermute(to_prev, 'ax', backward)  3.92 us
    pallas_call x1, Pallas kernels, shards(): pl.pallas_call(own_kernel, out_shape=shape(comps, planes, cells, wide), i...  2.44 us
  transfers between devices with their start and end apart: 8, of which 3 were waited for; matrix products, arithmetic and copies ran while one was open for 0% of the time, Pallas kernels for 5%

profile of v3, /device:TPU:6, one launch (start us, length us, event | category | flops | bytes accessed | tf_op | source)
XLA Modules:
  0.0 66.7 jit_solution(14030616125965609097)
XLA Ops:
  0.0 0.1 pad_add_fusion.info
  0.1 0.0 copy-start
  0.1 1.2 %copy-done = f32[4,4,8,2048]{3,2,1,0:T(8,128)S(1)} copy-done((f32[4,4,8,2048]{3,2,1,0:T(8,128)S(1)}, f32[4,4,8,2048]{3,2,1,0:T(8,128)}, u32[]{:S(2)}) %copy-start) | copy-done | bytes 1048600
  1.3 0.0 copy-start.1
  1.3 1.4 %pack_cross.1.crossing = f32[4,2,8,2048]{3,2,1,0:T(8,128)} custom-call(s32[3]{0:T(128)S(1)} %pad_add_fusion.info, f32[4,4,8,2048]{3,2,1,0:T(8,128)S(1)} %copy-done), custom_call_target="tpu_custom_call" | custom-call | tf_op jit(solution)/shard_map/pack_cross/pallas_call | solution.py:382
  2.7 0.0 copy-done.1
  2.7 1.0 %pack.1 = (f32[4,8,2048]{2,1,0:T(8,128)}, f32[4,8,2048]{2,1,0:T(8,128)S(1)}, f32[4,2,8,2048]{3,2,1,0:T(8,128)S(1)}, f32[4,2,8,2048]{3,2,1,0:T(8,128)S(1)}, f32[8,128]{1,0:T(8,128)S(1)}) custom-call(f32[4,4,8,2048]{3,2,1,0:T(8,128)S(1)} %copy-done.1, f32[4,2,8,2048]{3,2,1,0:T(8,128)} %pack_cross.1.crossing), custom_call_target="tpu_custom_call" | custom-call | tf_op jit(solution)/shard_map/pack/pallas_call | solution.py:391
  3.7 0.0 copy-start.5
  3.7 0.8 %copy-done.5 = f32[4,2,8,2048]{3,2,1,0:T(8,128)} copy-done((f32[4,2,8,2048]{3,2,1,0:T(8,128)}, f32[4,2,8,2048]{3,2,1,0:T(8,128)S(1)}, u32[]{:S(2)}) %copy-start.5) | copy-done | bytes 524312
  4.4 0.0 copy-start.4
  4.5 0.0 copy-start.2
  4.5 0.8 %broadcast_in_dim.3 = f32[64,8,128]{2,1,0:T(8,128)} broadcast(f32[8,128]{1,0:T(8,128)S(1)} %get-tuple-element.19), dimensions={1,2} | broadcast | bytes 266240 | tf_op jit(solution)/shard_map/broadcast_in_dim | solution.py:406
  5.2 13.5 %all-to-all-start = ((f32[64,8,128]{2,1,0:T(8,128)}), f32[64,8,128]{2,1,0:T(8,128)S(1)}, u32[]{:S(2)}, u32[]{:S(2)}) async-start(f32[64,8,128]{2,1,0:T(8,128)} %broadcast_in_dim.3), calls=%async_computation | async-start | bytes 524288 | tf_op jit(solution)/shard_map/all_to_all | solution.py:406
  18.8 8.1 %collective-permute-start = (f32[4,2,8,2048]{3,2,1,0:T(8,128)}, f32[4,2,8,2048]{3,2,1,0:T(8,128)S(1)}, u32[]{:S(2)}, u32[]{:S(2)}) collective-permute-start(f32[4,2,8,2048]{3,2,1,0:T(8,128)} %pack_cross.1.crossing), channel_id=1, source_target_pairs={{192,256},{256,192},{193,257},{257,193},{194,258},{258,194},{195,2... | collective-permute-start | bytes 1572872 | tf_op jit(solution)/shard_map/ppermute | solution.py:390
  26.9 1.3 %collective-permute-start.1 = (f32[4,2,8,2048]{3,2,1,0:T(8,128)}, f32[4,2,8,2048]{3,2,1,0:T(8,128)S(1)}, u32[]{:S(2)}, u32[]{:S(2)}) collective-permute-start(f32[4,2,8,2048]{3,2,1,0:T(8,128)} %copy-done.5), channel_id=1, source_target_pairs={{0,64},{64,128},{128,192},{256,320},{320,384},{384,448},{1,65},{65... | collective-permute-start | bytes 1572872 | tf_op jit(solution)/shard_map/ppermute | solution.py:401
  28.2 0.0 copy-done.4
  28.2 4.6 %collective-permute-start.2 = (f32[4,2,8,2048]{3,2,1,0:T(8,128)}, f32[4,2,8,2048]{3,2,1,0:T(8,128)S(1)}, u32[]{:S(2)}, u32[]{:S(2)}) collective-permute-start(f32[4,2,8,2048]{3,2,1,0:T(8,128)} %copy-done.4), channel_id=1, source_target_pairs={{64,0},{128,64},{192,128},{320,256},{384,320},{448,384},{65,1},{12... | collective-permute-start | bytes 1572872 | tf_op jit(solution)/shard_map/ppermute | solution.py:402
  32.8 1.9 %collective-permute-start.3 = (f32[4,8,2048]{2,1,0:T(8,128)}, f32[4,8,2048]{2,1,0:T(8,128)S(1)}, u32[]{:S(2)}, u32[]{:S(2)}) collective-permute-start(f32[4,8,2048]{2,1,0:T(8,128)} %get-tuple-element.17.up_msg), channel_id=1, source_target_pairs={{0,1},{1,2},{2,3},{3,4},{4,5},{5,6},{6,7},{7,8},{8,9},{9,10},{10,1... | collective-permute-start | bytes 786440 | tf_op jit(solution)/shard_map/ppermute | solution.py:403
  34.7 0.0 copy-done.2
  34.7 7.5 %collective-permute-start.4 = (f32[4,8,2048]{2,1,0:T(8,128)}, f32[4,8,2048]{2,1,0:T(8,128)S(1)}, u32[]{:S(2)}, u32[]{:S(2)}) collective-permute-start(f32[4,8,2048]{2,1,0:T(8,128)} %copy-done.2), channel_id=1, source_target_pairs={{1,0},{2,1},{3,2},{4,3},{5,4},{6,5},{7,6},{8,7},{9,8},{10,9},{11,1... | collective-permute-start | bytes 786440 | tf_op jit(solution)/shard_map/ppermute | solution.py:404
  43.0 0.1 pad_add_fusion.1.where_ref
  43.0 1.7 %collective-permute-done.3.left = f32[4,8,2048]{2,1,0:T(8,128)S(1)} collective-permute-done((f32[4,8,2048]{2,1,0:T(8,128)}, f32[4,8,2048]{2,1,0:T(8,128)S(1)}, u32[]{:S(2)}, u32[]{:S(2)}) %collective-permute-start.3) | collective-permute-done | bytes 262176 | tf_op jit(solution)/shard_map/ppermute | solution.py:403
  44.7 1.8 %collective-permute-done.4.right = f32[4,8,2048]{2,1,0:T(8,128)S(1)} collective-permute-done((f32[4,8,2048]{2,1,0:T(8,128)}, f32[4,8,2048]{2,1,0:T(8,128)S(1)}, u32[]{:S(2)}, u32[]{:S(2)}) %collective-permute-start.4) | collective-permute-done | bytes 262176 | tf_op jit(solution)/shard_map/ppermute | solution.py:404
  46.5 0.0 all-to-all-done.tiles
  46.5 0.6 pack_window.1
  47.1 1.9 %collective-permute-start.5 = (f32[8,2304]{1,0:T(8,128)S(1)}, f32[8,2304]{1,0:T(8,128)S(1)}, u32[]{:S(2)}, u32[]{:S(2)}) collective-permute-start(f32[8,2304]{1,0:T(8,128)S(1)} %get-tuple-element.22), channel_id=1, source_target_pairs={{0,64},{64,128},{128,192},{192,256},{256,320},{320,384},{384,448},... | collective-permute-start | bytes 221192 | tf_op jit(solution)/shard_map/ppermute | solution.py:415
  49.0 3.9 %collective-permute-start.6 = (f32[8,2304]{1,0:T(8,128)S(1)}, f32[8,2304]{1,0:T(8,128)S(1)}, u32[]{:S(2)}, u32[]{:S(2)}) collective-permute-start(f32[8,2304]{1,0:T(8,128)S(1)} %get-tuple-element.23), channel_id=1, source_target_pairs={{64,0},{128,64},{192,128},{256,192},{320,256},{384,320},{448,384},... | collective-permute-start | bytes 221192 | tf_op jit(solution)/shard_map/ppermute | solution.py:416
  53.6 0.0 collective-permute-done.crossed
  53.6 0.0 collective-permute-done.1.near_low
  53.6 0.0 collective-permute-done.2.near_high
  53.6 0.0 copy-start.3
  53.6 2.4 %own_section.1.sect = f32[4,4,8,2304]{3,2,1,0:T(8,128)S(1)} custom-call(s32[3]{0:T(128)S(1)} %pad_add_fusion.info, f32[1]{0:T(128)S(6)} %copy.5.frac, f32[4,4,8,2048]{3,2,1,0:T(8,128)S(1)} %copy-done.1, f32[4,2,8,2048]{3,2,1,0:T(8,128)S(1)} %collective-permute-done.crossed, f32[4,2,8,2048]{3,2,1,0:T(8,128)S(1)} %collective-permute-done.1.near_low, ...), custom_call_target="tpu_custom_call" | custom-call | flops 7864320 | bytes 3145728 | tf_op jit(solution)/shard_map/own_section/pallas_call | solution.py:420
  56.1 0.0 collective-permute-done.5.late_low
  56.1 5.2 %collective-permute-done.6.late_high = f32[8,2304]{1,0:T(8,128)S(1)} collective-permute-done((f32[8,2304]{1,0:T(8,128)S(1)}, f32[8,2304]{1,0:T(8,128)S(1)}, u32[]{:S(2)}, u32[]{:S(2)}) %collective-permute-start.6) | collective-permute-done | bytes 73760 | tf_op jit(solution)/shard_map/ppermute | solution.py:416
  61.3 0.0 copy-done.3
  61.3 5.5 %step.1 = f32[4,4,8,2048]{3,2,1,0:T(8,128)} custom-call(s32[3]{0:T(128)S(1)} %pad_add_fusion.info, f32[1]{0:T(128)S(6)} %copy.5.frac, f32[4,4,8,2048]{3,2,1,0:T(8,128)S(1)} %copy-done.1, f32[4,2,8,2048]{3,2,1,0:T(8,128)S(1)} %collective-permute-done.crossed, f32[4,2,8,2048]{3,2,1,0:T(8,128)S(1)} %collective-permute-done.1.near_low, ...), custom_call_target="tpu_custom_call" | custom-call | tf_op jit(solution)/shard_map/step/pallas_call | solution.py:433
Async XLA Ops:
  0.1 1.2 %copy-start = (f32[4,4,8,2048]{3,2,1,0:T(8,128)S(1)}, f32[4,4,8,2048]{3,2,1,0:T(8,128)}, u32[]{:S(2)}) copy-start(f32[4,4,8,2048]{3,2,1,0:T(8,128)} %st.7) | copy-start | bytes 3145732
  1.3 1.4 %copy-start.1 = (f32[4,4,8,2048]{3,2,1,0:T(8,128)S(1)}, f32[4,4,8,2048]{3,2,1,0:T(8,128)}, u32[]{:S(2)}) copy-start(f32[4,4,8,2048]{3,2,1,0:T(8,128)} %st.7) | copy-start | bytes 3145732
  3.7 0.8 %copy-start.5 = (f32[4,2,8,2048]{3,2,1,0:T(8,128)}, f32[4,2,8,2048]{3,2,1,0:T(8,128)S(1)}, u32[]{:S(2)}) copy-start(f32[4,2,8,2048]{3,2,1,0:T(8,128)S(1)} %get-tuple-element.15) | copy-start | bytes 1572868
  4.4 23.8 %copy-start.4 = (f32[4,2,8,2048]{3,2,1,0:T(8,128)}, f32[4,2,8,2048]{3,2,1,0:T(8,128)S(1)}, u32[]{:S(2)}) copy-start(f32[4,2,8,2048]{3,2,1,0:T(8,128)S(1)} %get-tuple-element.16) | copy-start | bytes 1572868
  4.5 30.3 %copy-start.2 = (f32[4,8,2048]{2,1,0:T(8,128)}, f32[4,8,2048]{2,1,0:T(8,128)S(1)}, u32[]{:S(2)}) copy-start(f32[4,8,2048]{2,1,0:T(8,128)S(1)} %get-tuple-element.18.dn_msg) | copy-start | bytes 786436
  5.2 41.3 %all-to-all-start = ((f32[64,8,128]{2,1,0:T(8,128)}), f32[64,8,128]{2,1,0:T(8,128)S(1)}, u32[]{:S(2)}, u32[]{:S(2)}) async-start(f32[64,8,128]{2,1,0:T(8,128)} %broadcast_in_dim.3), calls=%async_computation | async-start | bytes 524288 | tf_op jit(solution)/shard_map/all_to_all | solution.py:406
  18.8 34.8 %collective-permute-start = (f32[4,2,8,2048]{3,2,1,0:T(8,128)}, f32[4,2,8,2048]{3,2,1,0:T(8,128)S(1)}, u32[]{:S(2)}, u32[]{:S(2)}) collective-permute-start(f32[4,2,8,2048]{3,2,1,0:T(8,128)} %pack_cross.1.crossing), channel_id=1, source_target_pairs={{192,256},{256,192},{193,257},{257,193},{194,258},{258,194},{195,2... | collective-permute-start | bytes 1572872 | tf_op jit(solution)/shard_map/ppermute | solution.py:390
  26.9 26.7 %collective-permute-start.1 = (f32[4,2,8,2048]{3,2,1,0:T(8,128)}, f32[4,2,8,2048]{3,2,1,0:T(8,128)S(1)}, u32[]{:S(2)}, u32[]{:S(2)}) collective-permute-start(f32[4,2,8,2048]{3,2,1,0:T(8,128)} %copy-done.5), channel_id=1, source_target_pairs={{0,64},{64,128},{128,192},{256,320},{320,384},{384,448},{1,65},{65... | collective-permute-start | bytes 1572872 | tf_op jit(solution)/shard_map/ppermute | solution.py:401
  28.2 25.4 %collective-permute-start.2 = (f32[4,2,8,2048]{3,2,1,0:T(8,128)}, f32[4,2,8,2048]{3,2,1,0:T(8,128)S(1)}, u32[]{:S(2)}, u32[]{:S(2)}) collective-permute-start(f32[4,2,8,2048]{3,2,1,0:T(8,128)} %copy-done.4), channel_id=1, source_target_pairs={{64,0},{128,64},{192,128},{320,256},{384,320},{448,384},{65,1},{12... | collective-permute-start | bytes 1572872 | tf_op jit(solution)/shard_map/ppermute | solution.py:402
  32.8 11.9 %collective-permute-start.3 = (f32[4,8,2048]{2,1,0:T(8,128)}, f32[4,8,2048]{2,1,0:T(8,128)S(1)}, u32[]{:S(2)}, u32[]{:S(2)}) collective-permute-start(f32[4,8,2048]{2,1,0:T(8,128)} %get-tuple-element.17.up_msg), channel_id=1, source_target_pairs={{0,1},{1,2},{2,3},{3,4},{4,5},{5,6},{6,7},{7,8},{8,9},{9,10},{10,1... | collective-permute-start | bytes 786440 | tf_op jit(solution)/shard_map/ppermute | solution.py:403
  34.7 11.7 %collective-permute-start.4 = (f32[4,8,2048]{2,1,0:T(8,128)}, f32[4,8,2048]{2,1,0:T(8,128)S(1)}, u32[]{:S(2)}, u32[]{:S(2)}) collective-permute-start(f32[4,8,2048]{2,1,0:T(8,128)} %copy-done.2), channel_id=1, source_target_pairs={{1,0},{2,1},{3,2},{4,3},{5,4},{6,5},{7,6},{8,7},{9,8},{10,9},{11,1... | collective-permute-start | bytes 786440 | tf_op jit(solution)/shard_map/ppermute | solution.py:404
  47.1 9.0 %collective-permute-start.5 = (f32[8,2304]{1,0:T(8,128)S(1)}, f32[8,2304]{1,0:T(8,128)S(1)}, u32[]{:S(2)}, u32[]{:S(2)}) collective-permute-start(f32[8,2304]{1,0:T(8,128)S(1)} %get-tuple-element.22), channel_id=1, source_target_pairs={{0,64},{64,128},{128,192},{192,256},{256,320},{320,384},{384,448},... | collective-permute-start | bytes 221192 | tf_op jit(solution)/shard_map/ppermute | solution.py:415
  49.0 12.3 %collective-permute-start.6 = (f32[8,2304]{1,0:T(8,128)S(1)}, f32[8,2304]{1,0:T(8,128)S(1)}, u32[]{:S(2)}, u32[]{:S(2)}) collective-permute-start(f32[8,2304]{1,0:T(8,128)S(1)} %get-tuple-element.23), channel_id=1, source_target_pairs={{64,0},{128,64},{192,128},{256,192},{320,256},{384,320},{448,384},... | collective-permute-start | bytes 221192 | tf_op jit(solution)/shard_map/ppermute | solution.py:416
  53.6 7.7 %copy-start.3 = (f32[4,8,2048]{2,1,0:T(8,128)S(1)}, f32[4,8,2048]{2,1,0:T(8,128)}, u32[]{:S(2)}) copy-start(f32[4,8,2048]{2,1,0:T(8,128)} %copy-done.2) | copy-start | bytes 786436
